TPU v7x, 128 devices: a whole 4x4x4 slice. The times are simulated.
128 devices in a mesh: dp: 4 (over y), tm: 4 (over x), rows: 8 (over z, core).
Axes of the slice: x: 4, y: 4, z: 4, core: 2. Of those that a mesh axis runs over, the one named last changes fastest.
Arguments:
- latents: bfloat16 [4, 8, 32, 32, 384], P('dp', 'tm', 'rows'), may hold values from -6 to 6
- hidden: bfloat16 [4, 8, 32, 32, 384], P('dp', 'tm', 'rows'), may hold values from -8 to 8
- cotangent: bfloat16 [4, 8, 32, 32, 384], P('dp', 'tm', 'rows'), may hold values from -6 to 6
- conv_one: bfloat16 [3, 3, 3, 384, 384], replicated, may hold values from -0.0625 to 0.0625
- conv_two: bfloat16 [3, 3, 3, 384, 384], replicated, may hold values from -0.0625 to 0.0625
- lengths: int32 [4], P('dp'), may hold values from 3 to 8, as said below
Outputs:
- latent_grad: float32 [4, 8, 32, 32, 384], P('dp', None, None, ('tm', 'rows'))
Inputs may be any that keep to these rules, and one draw needn't show every extreme that they name: `lengths`: at least one clip has all 8 frames valid.
All inputs are finite; a program needn't handle non-finite values.
Results may differ from a plain program's by a relative error of at most 0.00092.
Values may be sent and summed in bfloat16 or wider, within the bound.
A program may use at most 64 MiB of HBM per device.

v0:
```python
import jax
import jax.numpy as jnp
from jax import lax
from jax.sharding import PartitionSpec as P


def with_halo(block, sides, width):
    for axis, dim in sides:
        count = lax.axis_size(axis)
        forward = [(i, i + 1) for i in range(count - 1)]
        backward = [(target, source) for source, target in forward]
        low = lax.ppermute(
            lax.slice_in_dim(block, block.shape[dim] - width, None, axis=dim), axis, forward
        )
        high = lax.ppermute(lax.slice_in_dim(block, 0, width, axis=dim), axis, backward)
        block = jnp.concatenate([low, block, high], axis=dim)
    return block


def shifted(value, axis, by):
    devices = lax.axis_size(axis)
    pairs = [(i, i + by) for i in range(devices) if 0 <= i + by < devices]
    return lax.ppermute(value, axis, pairs)


def silu_slope(values):
    sigmoid_of = jax.nn.sigmoid(values)
    return sigmoid_of * (1.0 + values * (1.0 - sigmoid_of))


def extended(row_band, next_frames):
    joined = jnp.concatenate([row_band, next_frames], axis=0)
    return jnp.pad(joined, ((0, 0), (0, 0), (1, 1), (0, 0)))


def transposed_conv(padded, kernel, frame_count, row_count, col_count):
    summed = jnp.zeros((frame_count, row_count, col_count, kernel.shape[4]), jnp.float32)
    for time_tap in range(3):
        for row_tap in range(3):
            slab_rows = padded[time_tap : time_tap + frame_count, row_tap : row_tap + row_count]
            stacked = jnp.stack(
                [slab_rows[:, :, col_tap : col_tap + col_count] for col_tap in range(3)], axis=3
            )
            kernel_slice = kernel[2 - time_tap, 2 - row_tap, ::-1]
            summed = summed + jnp.einsum(
                "frwkc,kdc->frwd", stacked, kernel_slice, preferred_element_type=jnp.float32
            )
    return summed


def on_device(latents, hidden, cotangent, conv_one, conv_two, lengths):
    frame_dev = latents.shape[1]
    row_dev = latents.shape[2]
    col_count = latents.shape[3]
    first_frame = lax.axis_index("tm") * frame_dev
    frames = first_frame + jnp.arange(frame_dev, dtype=jnp.int32)
    live_frames = frames < lengths[0]
    masked = jnp.where(live_frames[:, None, None, None], cotangent[0], jnp.zeros_like(cotangent[0]))
    cot_band = with_halo(masked, (("rows", 1),), 1)
    cot_next = shifted(cot_band, "tm", -1)
    grad_act = transposed_conv(
        extended(cot_band, cot_next), conv_two, frame_dev, row_dev, col_count
    )
    grad_hidden = (grad_act * silu_slope(hidden[0].astype(jnp.float32))).astype(jnp.bfloat16)
    hidden_band = with_halo(grad_hidden, (("rows", 1),), 1)
    hidden_next = shifted(hidden_band, "tm", -1)
    grad_input = transposed_conv(
        extended(hidden_band, hidden_next), conv_one, frame_dev, row_dev, col_count
    )
    result = masked.astype(jnp.float32) + grad_input * silu_slope(latents[0].astype(jnp.float32))
    result = result[None]
    return lax.all_to_all(
        lax.all_to_all(result, "tm", split_axis=3, concat_axis=1, tiled=True),
        "rows",
        split_axis=3,
        concat_axis=2,
        tiled=True,
    )


def solution(mesh):
    in_specs = (
        P("dp", "tm", "rows", None, None),
        P("dp", "tm", "rows", None, None),
        P("dp", "tm", "rows", None, None),
        P(),
        P(),
        P("dp"),
    )
    out_specs = P("dp", None, None, ("tm", "rows"), None)
    return jax.shard_map(
        on_device, mesh=mesh, in_specs=in_specs, out_specs=out_specs, check_vma=False
    )
```

profile of v0, /device:TPU:1, one launch (start us, length us, event | category | flops | bytes accessed | tf_op | source)
XLA Modules:
  0.0 109.8 jit_solution(15612592361012000791)
XLA Ops:
  0.7 1.0 bitcast_select_fusion.1
  1.7 4.9 %collective-permute-start = (bf16[2,1,32,384]{3,2,1,0:T(8,128)(2,1)S(1)}, bf16[2,1,32,384]{3,2,1,0:T(8,128)(2,1)S(1)}, u32[]{:S(2)}, u32[]{:S(2)}) collective-permute-start(bf16[2,1,32,384]{3,2,1,0:T(8,128)(2,1)S(1)} %get-tuple-element.77), channel_id=1, source_target_pairs={{0,1},{1,2},{2,3},{3,4},{4,5},{5,6},{6,7},{8,9},{9,10},{10,11},{11... | collective-permute-start | bytes 147464 | tf_op jit(solution)/shard_map/ppermute | solution.py:12
  6.7 1.9 %collective-permute-start.1 = (bf16[2,1,32,384]{3,2,1,0:T(8,128)(2,1)S(1)}, bf16[2,1,32,384]{3,2,1,0:T(8,128)(2,1)S(1)}, u32[]{:S(2)}, u32[]{:S(2)}) collective-permute-start(bf16[2,1,32,384]{3,2,1,0:T(8,128)(2,1)S(1)} %get-tuple-element.78), channel_id=1, source_target_pairs={{1,0},{2,1},{3,2},{4,3},{5,4},{6,5},{7,6},{9,8},{10,9},{11,10},{12... | collective-permute-start | bytes 147464 | tf_op jit(solution)/shard_map/ppermute | solution.py:15
  8.6 5.3 %fusion.105 = (bf16[1,1,3,384,384]{4,3,2,1,0:T(8,128)(2,1)}, bf16[1,1,3,384,384]{4,3,2,1,0:T(8,128)(2,1)S(1)}, bf16[1,1,3,384,384]{4,3,2,1,0:T(8,128)(2,1)S(1)},...) fusion(bf16[3,3,3,384,384]{4,3,2,1,0:T(8,128)(2,1)} %param.10), kind=kLoop, calls=%fused_computation.212 | loop fusion | bytes 15925248 | tf_op jit(solution)/shard_map/slice | solution.py:44
  13.9 2.2 %rev.55 = bf16[1,1,3,384,384]{4,3,2,1,0:T(8,128)(2,1)} reverse(bf16[1,1,3,384,384]{4,3,2,1,0:T(8,128)(2,1)} %get-tuple-element.14), dimensions={2} | reverse | bytes 1769472 | tf_op jit(solution)/shard_map/rev | solution.py:44
  16.1 2.2 %rev.56 = bf16[1,1,3,384,384]{4,3,2,1,0:T(8,128)(2,1)} reverse(bf16[1,1,3,384,384]{4,3,2,1,0:T(8,128)(2,1)} %get-tuple-element.19), dimensions={2} | reverse | bytes 1769472 | tf_op jit(solution)/shard_map/rev | solution.py:44
  18.3 2.2 %rev.57 = bf16[1,1,3,384,384]{4,3,2,1,0:T(8,128)(2,1)} reverse(bf16[1,1,3,384,384]{4,3,2,1,0:T(8,128)(2,1)} %get-tuple-element.18), dimensions={2} | reverse | bytes 1769472 | tf_op jit(solution)/shard_map/rev | solution.py:44
  20.5 2.2 %rev.58 = bf16[1,1,3,384,384]{4,3,2,1,0:T(8,128)(2,1)} reverse(bf16[1,1,3,384,384]{4,3,2,1,0:T(8,128)(2,1)} %get-tuple-element.17), dimensions={2} | reverse | bytes 1769472 | tf_op jit(solution)/shard_map/rev | solution.py:44
  22.7 1.0 rev.59
  23.9 1.3 %rev.62 = bf16[1,1,3,384,384]{4,3,2,1,0:T(8,128)(2,1)S(1)} reverse(bf16[1,1,3,384,384]{4,3,2,1,0:T(8,128)(2,1)} %get-tuple-element.21), dimensions={2} | reverse | bytes 1769472 | tf_op jit(solution)/shard_map/rev | solution.py:44
  25.1 2.2 %rev.54 = bf16[1,1,3,384,384]{4,3,2,1,0:T(8,128)(2,1)} reverse(bf16[1,1,3,384,384]{4,3,2,1,0:T(8,128)(2,1)} %get-tuple-element.20), dimensions={2} | reverse | bytes 1769472 | tf_op jit(solution)/shard_map/rev | solution.py:44
  27.4 1.4 %collective-permute-start.2 = (bf16[2,6,32,384]{3,2,1,0:T(8,128)(2,1)S(1)}, bf16[2,6,32,384]{3,2,1,0:T(8,128)(2,1)S(1)}, u32[]{:S(2)}, u32[]{:S(2)}) collective-permute-start(bf16[2,6,32,384]{3,2,1,0:T(8,128)(2,1)S(1)} %pad_maximum_fusion.19), channel_id=1, source_target_pairs={{8,0},{16,8},{24,16},{9,1},{17,9},{25,17},{10,2},{18,10},{26,18},{... | collective-permute-start | bytes 884744 | tf_op jit(solution)/shard_map/ppermute | solution.py:23
  29.0 6.8 %collective-permute-done.2 = bf16[2,6,32,384]{3,2,1,0:T(8,128)(2,1)S(1)} collective-permute-done((bf16[2,6,32,384]{3,2,1,0:T(8,128)(2,1)S(1)}, bf16[2,6,32,384]{3,2,1,0:T(8,128)(2,1)S(1)}, u32[]{:S(2)}, u32[]{:S(2)}) %collective-permute-start.2) | collective-permute-done | bytes 294944 | tf_op jit(solution)/shard_map/ppermute | solution.py:23
  42.1 6.5 %collective-permute-start.3 = (bf16[2,1,32,384]{3,2,1,0:T(8,128)(2,1)S(1)}, bf16[2,1,32,384]{3,2,1,0:T(8,128)(2,1)S(1)}, u32[]{:S(2)}, u32[]{:S(2)}) collective-permute-start(bf16[2,1,32,384]{3,2,1,0:T(8,128)(2,1)S(1)} %get-tuple-element.73), channel_id=1, source_target_pairs={{0,1},{1,2},{2,3},{3,4},{4,5},{5,6},{6,7},{8,9},{9,10},{10,11},{11... | collective-permute-start | bytes 147464 | tf_op jit(solution)/shard_map/ppermute | solution.py:12
  48.6 1.9 %collective-permute-start.4 = (bf16[2,1,32,384]{3,2,1,0:T(8,128)(2,1)S(1)}, bf16[2,1,32,384]{3,2,1,0:T(8,128)(2,1)S(1)}, u32[]{:S(2)}, u32[]{:S(2)}) collective-permute-start(bf16[2,1,32,384]{3,2,1,0:T(8,128)(2,1)S(1)} %get-tuple-element.74), channel_id=1, source_target_pairs={{1,0},{2,1},{3,2},{4,3},{5,4},{6,5},{7,6},{9,8},{10,9},{11,10},{12... | collective-permute-start | bytes 147464 | tf_op jit(solution)/shard_map/ppermute | solution.py:15
  50.6 3.5 %collective-permute-done.4 = bf16[2,1,32,384]{3,2,1,0:T(8,128)(2,1)S(1)} collective-permute-done((bf16[2,1,32,384]{3,2,1,0:T(8,128)(2,1)S(1)}, bf16[2,1,32,384]{3,2,1,0:T(8,128)(2,1)S(1)}, u32[]{:S(2)}, u32[]{:S(2)}) %collective-permute-start.4) | collective-permute-done | bytes 49184 | tf_op jit(solution)/shard_map/ppermute | solution.py:15
  54.8 1.5 %collective-permute-start.5 = (bf16[2,6,32,384]{3,2,1,0:T(8,128)(2,1)}, bf16[2,6,32,384]{3,2,1,0:T(8,128)(2,1)}, u32[]{:S(2)}, u32[]{:S(2)}) collective-permute-start(bf16[2,6,32,384]{3,2,1,0:T(8,128)(2,1)} %pad_maximum_fusion.20), channel_id=1, source_target_pairs={{8,0},{16,8},{24,16},{9,1},{17,9},{25,17},{10,2},{18,10},{26,18},{... | collective-permute-start | bytes 884744 | tf_op jit(solution)/shard_map/ppermute | solution.py:23
  56.3 2.7 %fusion.104 = (bf16[1,1,3,384,384]{4,3,2,1,0:T(8,128)(2,1)}, bf16[1,1,3,384,384]{4,3,2,1,0:T(8,128)(2,1)S(1)}, bf16[1,1,3,384,384]{4,3,2,1,0:T(8,128)(2,1)S(1)},...) fusion(bf16[3,3,3,384,384]{4,3,2,1,0:T(8,128)(2,1)S(1)} %bitcas, ...), kind=kLoop, calls=%fused_computation.211 | loop fusion | bytes 15925248 | tf_op jit(solution)/shard_map/slice | solution.py:44
  59.0 2.2 %rev.63 = bf16[1,1,3,384,384]{4,3,2,1,0:T(8,128)(2,1)} reverse(bf16[1,1,3,384,384]{4,3,2,1,0:T(8,128)(2,1)} %get-tuple-element.5), dimensions={2} | reverse | bytes 1769472 | tf_op jit(solution)/shard_map/rev | solution.py:44
  61.2 2.2 %rev.64 = bf16[1,1,3,384,384]{4,3,2,1,0:T(8,128)(2,1)} reverse(bf16[1,1,3,384,384]{4,3,2,1,0:T(8,128)(2,1)} %get-tuple-element.11), dimensions={2} | reverse | bytes 1769472 | tf_op jit(solution)/shard_map/rev | solution.py:44
  63.4 2.2 %rev.65 = bf16[1,1,3,384,384]{4,3,2,1,0:T(8,128)(2,1)} reverse(bf16[1,1,3,384,384]{4,3,2,1,0:T(8,128)(2,1)} %get-tuple-element.10), dimensions={2} | reverse | bytes 1769472 | tf_op jit(solution)/shard_map/rev | solution.py:44
  65.6 2.2 %rev.66 = bf16[1,1,3,384,384]{4,3,2,1,0:T(8,128)(2,1)} reverse(bf16[1,1,3,384,384]{4,3,2,1,0:T(8,128)(2,1)} %get-tuple-element.9), dimensions={2} | reverse | bytes 1769472 | tf_op jit(solution)/shard_map/rev | solution.py:44
  67.7 2.2 %rev.67 = bf16[1,1,3,384,384]{4,3,2,1,0:T(8,128)(2,1)} reverse(bf16[1,1,3,384,384]{4,3,2,1,0:T(8,128)(2,1)} %get-tuple-element.8), dimensions={2} | reverse | bytes 1769472 | tf_op jit(solution)/shard_map/rev | solution.py:44
  69.9 1.0 rev.68
  71.0 1.0 rev.69
  72.2 1.2 %fusion.100 = (bf16[2,4,32,1,384]{4,2,1,0,3:T(8,128)(2,1)S(1)}, bf16[2,4,32,1,384]{4,2,1,0,3:T(8,128)(2,1)S(1)}) fusion(bf16[2,4,32,384]{3,2,1,0:T(8,128)(2,1)} %copy-done.5, bf16[2,1,32,384]{3,2,1,0:T(8,128)(2,1)} %copy-done.16, bf16[2,1,32,384]{3,2,1,0:T(8,128)(2,1)} %copy-done.17), kind=kLoop, calls=%fused_computation.196 | loop fusion | flops 196608 | bytes 688128 | tf_op jit(solution)/shard_map/stack | solution.py:41
  73.4 1.1 %pad_maximum_fusion.9 = bf16[4,6,32,384]{3,2,1,0:T(8,128)(2,1)S(1)} fusion(bf16[2,6,32,384]{3,2,1,0:T(8,128)(2,1)} %collective-permute-done.5, bf16[2,1,32,384]{3,2,1,0:T(8,128)(2,1)} %copy-done.17, bf16[2,4,32,384]{3,2,1,0:T(8,128)(2,1)} %copy-done.5, bf16[2,1,32,384]{3,2,1,0:T(8,128)(2,1)} %copy-done.16), kind=kLoop, calls=%fused_computation.60 | loop fusion | flops 884736 | bytes 1179648 | tf_op jit(solution)/shard_map/concatenate | solution.py:32
  75.3 1.7 %convolution_bitcast_fusion.8 = f32[2,4,32,384]{3,2,0,1:T(8,128)S(1)} fusion(bf16[1,1,3,384,384]{4,3,2,1,0:T(8,128)(2,1)} %rev.63, bf16[2,4,32,1,384]{4,2,1,0,3:T(8,128)(2,1)S(1)} %get-tuple-element.24, bf16[2,4,32,1,384]{4,2,1,0,3:T(8,128)(2,1)S(1)} %get-tuple-element.71, bf16[2,4,32,1,384]{4,2,1,0,3:T(8,128)(2,1)S(1)} %get-tuple-element.23), kind=kOutput, calls=%fused_computation.8 | convolution fusion | flops 227082240 | bytes 1867776 | tf_op jit(solution)/shard_map/frwkc,kdc->frwd/dot_general | solution.py:45
  79.6 1.2 %slice_bitcast_fusion.2 = (bf16[2,4,32,1,384]{4,2,1,0,3:T(8,128)(2,1)S(1)}, bf16[2,4,32,1,384]{4,2,1,0,3:T(8,128)(2,1)S(1)}, bf16[2,4,32,1,384]{4,2,1,0,3:T(8,128)(2,1)S(1)}) fusion(bf16[2,6,32,384]{3,2,1,0:T(8,128)(2,1)} %collective-permute-done.5), kind=kLoop, calls=%fused_computation.189 | loop fusion | bytes 1179648 | tf_op jit(solution)/shard_map/stack | solution.py:41
  83.0 12.3 %all_to_all.36 = f32[1,2,4,32,384]{4,2,1,0,3:T(4,128)S(1)} all-to-all(f32[1,2,4,32,384]{4,2,1,0,3:T(4,128)S(1)} %copy.127), channel_id=1, replica_groups=mesh['dp'=4,'tm'=4,'rows'=8] {'tm'}, dimensions={3} | all-to-all | bytes 786432 | tf_op jit(solution)/shard_map/all_to_all | solution.py:73
  95.5 13.1 %all_to_all.37 = f32[1,8,4,8,384]{4,2,1,0,3:T(4,128)S(1)} all-to-all(f32[1,8,4,8,384]{4,2,1,0,3:T(4,128)S(1)} %copy.130), channel_id=1, replica_groups=mesh['dp'=4,'tm'=4,'rows'=8] {'rows'}, dimensions={3} | all-to-all | bytes 786432 | tf_op jit(solution)/shard_map/all_to_all | solution.py:72
  108.7 1.2 %copy.132 = f32[1,8,32,1,384]{4,3,2,1,0:T(1,128)} copy(f32[1,8,32,1,384]{4,1,2,3,0:T(8,128)S(1)} %bitcast.324) | data formatting | bytes 786432 | tf_op jit(solution)/shard_map/all_to_all | solution.py:72
  (93 shorter events, 13.0 us)
Async XLA Ops:
  1.7 25.6 %collective-permute-start = (bf16[2,1,32,384]{3,2,1,0:T(8,128)(2,1)S(1)}, bf16[2,1,32,384]{3,2,1,0:T(8,128)(2,1)S(1)}, u32[]{:S(2)}, u32[]{:S(2)}) collective-permute-start(bf16[2,1,32,384]{3,2,1,0:T(8,128)(2,1)S(1)} %get-tuple-element.77), channel_id=1, source_target_pairs={{0,1},{1,2},{2,3},{3,4},{4,5},{5,6},{6,7},{8,9},{9,10},{10,11},{11... | collective-permute-start | bytes 147464 | tf_op jit(solution)/shard_map/ppermute | solution.py:12
  6.7 20.7 %collective-permute-start.1 = (bf16[2,1,32,384]{3,2,1,0:T(8,128)(2,1)S(1)}, bf16[2,1,32,384]{3,2,1,0:T(8,128)(2,1)S(1)}, u32[]{:S(2)}, u32[]{:S(2)}) collective-permute-start(bf16[2,1,32,384]{3,2,1,0:T(8,128)(2,1)S(1)} %get-tuple-element.78), channel_id=1, source_target_pairs={{1,0},{2,1},{3,2},{4,3},{5,4},{6,5},{7,6},{9,8},{10,9},{11,10},{12... | collective-permute-start | bytes 147464 | tf_op jit(solution)/shard_map/ppermute | solution.py:15
  13.9 14.9 %copy-start.7 = (bf16[1,2,4,32,384]{4,3,2,1,0:T(8,128)(2,1)S(1)}, bf16[1,2,4,32,384]{4,3,2,1,0:T(8,128)(2,1)}, u32[]{:S(2)}) copy-start(bf16[1,2,4,32,384]{4,3,2,1,0:T(8,128)(2,1)} %param.8) | copy-start | bytes 589828
  27.3 9.5 %copy-start.4 = (bf16[1,1,3,384,384]{4,3,2,1,0:T(8,128)(2,1)S(1)}, bf16[1,1,3,384,384]{4,3,2,1,0:T(8,128)(2,1)}, u32[]{:S(2)}) copy-start(bf16[1,1,3,384,384]{4,3,2,1,0:T(8,128)(2,1)} %rev.55) | copy-start | bytes 2654212
  27.3 10.0 %copy-start.3 = (bf16[1,1,3,384,384]{4,3,2,1,0:T(8,128)(2,1)S(1)}, bf16[1,1,3,384,384]{4,3,2,1,0:T(8,128)(2,1)}, u32[]{:S(2)}) copy-start(bf16[1,1,3,384,384]{4,3,2,1,0:T(8,128)(2,1)} %rev.56) | copy-start | bytes 2654212
  27.4 8.4 %collective-permute-start.2 = (bf16[2,6,32,384]{3,2,1,0:T(8,128)(2,1)S(1)}, bf16[2,6,32,384]{3,2,1,0:T(8,128)(2,1)S(1)}, u32[]{:S(2)}, u32[]{:S(2)}) collective-permute-start(bf16[2,6,32,384]{3,2,1,0:T(8,128)(2,1)S(1)} %pad_maximum_fusion.19), channel_id=1, source_target_pairs={{8,0},{16,8},{24,16},{9,1},{17,9},{25,17},{10,2},{18,10},{26,18},{... | collective-permute-start | bytes 884744 | tf_op jit(solution)/shard_map/ppermute | solution.py:23
  28.9 9.0 %copy-start.2 = (bf16[1,1,3,384,384]{4,3,2,1,0:T(8,128)(2,1)S(1)}, bf16[1,1,3,384,384]{4,3,2,1,0:T(8,128)(2,1)}, u32[]{:S(2)}) copy-start(bf16[1,1,3,384,384]{4,3,2,1,0:T(8,128)(2,1)} %rev.57) | copy-start | bytes 2654212
  35.9 2.6 %copy-start.1 = (bf16[1,1,3,384,384]{4,3,2,1,0:T(8,128)(2,1)S(1)}, bf16[1,1,3,384,384]{4,3,2,1,0:T(8,128)(2,1)}, u32[]{:S(2)}) copy-start(bf16[1,1,3,384,384]{4,3,2,1,0:T(8,128)(2,1)} %rev.58) | copy-start | bytes 2654212
  36.6 2.6 %copy-start = (bf16[1,1,3,384,384]{4,3,2,1,0:T(8,128)(2,1)S(1)}, bf16[1,1,3,384,384]{4,3,2,1,0:T(8,128)(2,1)}, u32[]{:S(2)}) copy-start(bf16[1,1,3,384,384]{4,3,2,1,0:T(8,128)(2,1)} %rev.59) | copy-start | bytes 2654212
  38.5 3.0 %copy-start.9 = (bf16[1,1,3,384,384]{4,3,2,1,0:T(8,128)(2,1)S(1)}, bf16[1,1,3,384,384]{4,3,2,1,0:T(8,128)(2,1)}, u32[]{:S(2)}) copy-start(bf16[1,1,3,384,384]{4,3,2,1,0:T(8,128)(2,1)} %rev.54) | copy-start | bytes 2654212
  38.5 3.0 %copy-start.19 = (bf16[1,2,4,32,384]{4,3,2,1,0:T(8,128)(2,1)S(1)}, bf16[1,2,4,32,384]{4,3,2,1,0:T(8,128)(2,1)}, u32[]{:S(2)}) copy-start(bf16[1,2,4,32,384]{4,3,2,1,0:T(8,128)(2,1)} %param.7) | copy-start | bytes 589828
  39.7 16.6 %slice-start = ((s8[7962624]{0:T(1024)(128)(4,1)}), s8[4194304]{0:T(1024)(128)(4,1)S(1)}, s32[]{:S(2)}) async-start(s8[7962624]{0:T(1024)(128)(4,1)} %bitcast.319), calls=%async_computation.2 | async-start | bytes 8388608
  40.9 15.4 %slice-start.1 = ((s8[7962624]{0:T(1024)(128)(4,1)}), s8[3768320]{0:T(1024)(128)(4,1)S(1)}, s32[]{:S(2)}) async-start(s8[7962624]{0:T(1024)(128)(4,1)} %bitcast.319), calls=%async_computation.3 | async-start | bytes 7536640
  42.1 12.7 %copy-start.5 = (bf16[2,4,32,384]{3,2,1,0:T(8,128)(2,1)}, bf16[2,4,32,384]{3,2,1,0:T(8,128)(2,1)S(1)}, u32[]{:S(2)}) copy-start(bf16[2,4,32,384]{3,2,1,0:T(8,128)(2,1)S(1)} %fusion.9) | copy-start | bytes 589828
  42.1 8.4 %collective-permute-start.3 = (bf16[2,1,32,384]{3,2,1,0:T(8,128)(2,1)S(1)}, bf16[2,1,32,384]{3,2,1,0:T(8,128)(2,1)S(1)}, u32[]{:S(2)}, u32[]{:S(2)}) collective-permute-start(bf16[2,1,32,384]{3,2,1,0:T(8,128)(2,1)S(1)} %get-tuple-element.73), channel_id=1, source_target_pairs={{0,1},{1,2},{2,3},{3,4},{4,5},{5,6},{6,7},{8,9},{9,10},{10,11},{11... | collective-permute-start | bytes 147464 | tf_op jit(solution)/shard_map/ppermute | solution.py:12
  48.6 5.4 %collective-permute-start.4 = (bf16[2,1,32,384]{3,2,1,0:T(8,128)(2,1)S(1)}, bf16[2,1,32,384]{3,2,1,0:T(8,128)(2,1)S(1)}, u32[]{:S(2)}, u32[]{:S(2)}) collective-permute-start(bf16[2,1,32,384]{3,2,1,0:T(8,128)(2,1)S(1)} %get-tuple-element.74), channel_id=1, source_target_pairs={{1,0},{2,1},{3,2},{4,3},{5,4},{6,5},{7,6},{9,8},{10,9},{11,10},{12... | collective-permute-start | bytes 147464 | tf_op jit(solution)/shard_map/ppermute | solution.py:15
  50.6 4.2 %copy-start.16 = (bf16[2,1,32,384]{3,2,1,0:T(8,128)(2,1)}, bf16[2,1,32,384]{3,2,1,0:T(8,128)(2,1)S(1)}, u32[]{:S(2)}) copy-start(bf16[2,1,32,384]{3,2,1,0:T(8,128)(2,1)S(1)} %collective-permute-done.3) | copy-start | bytes 147460
  54.0 0.8 copy-start.17
  54.8 18.6 %collective-permute-start.5 = (bf16[2,6,32,384]{3,2,1,0:T(8,128)(2,1)}, bf16[2,6,32,384]{3,2,1,0:T(8,128)(2,1)}, u32[]{:S(2)}, u32[]{:S(2)}) collective-permute-start(bf16[2,6,32,384]{3,2,1,0:T(8,128)(2,1)} %pad_maximum_fusion.20), channel_id=1, source_target_pairs={{8,0},{16,8},{24,16},{9,1},{17,9},{25,17},{10,2},{18,10},{26,18},{... | collective-permute-start | bytes 884744 | tf_op jit(solution)/shard_map/ppermute | solution.py:23
  71.0 6.0 %copy-start.6 = (bf16[2,4,32,384]{3,2,1,0:T(8,128)(2,1)S(1)}, bf16[2,4,32,384]{3,2,1,0:T(8,128)(2,1)}, u32[]{:S(2)}) copy-start(bf16[2,4,32,384]{3,2,1,0:T(8,128)(2,1)} %copy-done.5) | copy-start | bytes 589828
  72.2 4.8 %copy-start.15 = (bf16[1,1,3,384,384]{4,3,2,1,0:T(8,128)(2,1)S(1)}, bf16[1,1,3,384,384]{4,3,2,1,0:T(8,128)(2,1)}, u32[]{:S(2)}) copy-start(bf16[1,1,3,384,384]{4,3,2,1,0:T(8,128)(2,1)} %rev.64) | copy-start | bytes 2654212
  72.2 5.4 %copy-start.14 = (bf16[1,1,3,384,384]{4,3,2,1,0:T(8,128)(2,1)S(1)}, bf16[1,1,3,384,384]{4,3,2,1,0:T(8,128)(2,1)}, u32[]{:S(2)}) copy-start(bf16[1,1,3,384,384]{4,3,2,1,0:T(8,128)(2,1)} %rev.65) | copy-start | bytes 2654212
  72.2 5.8 %copy-start.13 = (bf16[1,1,3,384,384]{4,3,2,1,0:T(8,128)(2,1)S(1)}, bf16[1,1,3,384,384]{4,3,2,1,0:T(8,128)(2,1)}, u32[]{:S(2)}) copy-start(bf16[1,1,3,384,384]{4,3,2,1,0:T(8,128)(2,1)} %rev.66) | copy-start | bytes 2654212
  74.5 4.0 %copy-start.12 = (bf16[1,1,3,384,384]{4,3,2,1,0:T(8,128)(2,1)S(1)}, bf16[1,1,3,384,384]{4,3,2,1,0:T(8,128)(2,1)}, u32[]{:S(2)}) copy-start(bf16[1,1,3,384,384]{4,3,2,1,0:T(8,128)(2,1)} %rev.67) | copy-start | bytes 2654212
  75.2 3.9 %copy-start.11 = (bf16[1,1,3,384,384]{4,3,2,1,0:T(8,128)(2,1)S(1)}, bf16[1,1,3,384,384]{4,3,2,1,0:T(8,128)(2,1)}, u32[]{:S(2)}) copy-start(bf16[1,1,3,384,384]{4,3,2,1,0:T(8,128)(2,1)} %rev.68) | copy-start | bytes 2654212
  77.0 3.7 %copy-start.10 = (bf16[1,1,3,384,384]{4,3,2,1,0:T(8,128)(2,1)S(1)}, bf16[1,1,3,384,384]{4,3,2,1,0:T(8,128)(2,1)}, u32[]{:S(2)}) copy-start(bf16[1,1,3,384,384]{4,3,2,1,0:T(8,128)(2,1)} %rev.69) | copy-start | bytes 2654212
  78.6 3.7 %copy-start.8 = (bf16[1,2,4,32,384]{4,3,2,1,0:T(8,128)(2,1)S(1)}, bf16[1,2,4,32,384]{4,3,2,1,0:T(8,128)(2,1)}, u32[]{:S(2)}) copy-start(bf16[1,2,4,32,384]{4,3,2,1,0:T(8,128)(2,1)} %param.8) | copy-start | bytes 589828
  78.6 3.7 %copy-start.18 = (bf16[1,2,4,32,384]{4,3,2,1,0:T(8,128)(2,1)S(1)}, bf16[1,2,4,32,384]{4,3,2,1,0:T(8,128)(2,1)}, u32[]{:S(2)}) copy-start(bf16[1,2,4,32,384]{4,3,2,1,0:T(8,128)(2,1)} %param.6) | copy-start | bytes 589828
where the time goes:
time: 111 us; the launch traced here: 110 us
  local copies, waits for them, and re-layouts  39 us (35%)
  blocking collectives  25.5 us (23%)
  starting transfers between devices  18.2 us (16%)
  waiting for transfers between devices  10.3 us (9%)
  matrix products  10.2 us (9%)
  other arithmetic  5.43 us (5%)
  between operations  1.36 us (1%)
    rev x18, local copies, waits for them, and re-layouts, transposed_conv(): kernel_slice = kernel[2 - time_tap, 2 - row_tap, ::-1]  26.5 us
    all_to_all x1, blocking collectives, on_device(): lax.all_to_all(lax.all_to_all(result, 'tm', split_axis=3, concat_axis=1,...  13.1 us
    all_to_all x1, blocking collectives, on_device(): lax.all_to_all(result, 'tm', split_axis=3, concat_axis=1, tiled=True)  12.3 us
    ppermute x2, starting transfers between devices, with_halo(): lax.ppermute(lax.slice_in_dim(block, block.shape[dim] - width, None, axis...  11.4 us
    dot_general x18, matrix products, transposed_conv(): jnp.einsum('frwkc,kdc->frwd', stacked, kernel_slice, preferred_element_ty...  10.2 us
    slice x2, local copies, waits for them, and re-layouts, transposed_conv(): kernel_slice = kernel[2 - time_tap, 2 - row_tap, ::-1]  8.04 us
    ppermute x2, waiting for transfers between devices, shifted(): return lax.ppermute(value, axis, pairs)  6.78 us
    ppermute x2, starting transfers between devices, with_halo(): lax.ppermute(lax.slice_in_dim(block, 0, width, axis=dim), axis, backward)  3.84 us
  transfers between devices with their start and end apart: 6, of which 2 were waited for; matrix products, arithmetic and copies ran while one was open for 33% of the time, Pallas kernels for 0%

commit v1 on v0

v1 whole, which is shorter than its diff:
```python
import functools

import jax
import jax.numpy as jnp
from jax import lax
from jax.experimental import pallas as pl
from jax.experimental.pallas import tpu as pltpu
from jax.sharding import PartitionSpec as P

MESH = pl.DeviceIdType.MESH
NT = (((1,), (1,)), ((), ()))
F32 = jnp.float32
BF16 = jnp.bfloat16
SPLIT = 256


def silu_slope(values):
    gate = 1.0 / (1.0 + jnp.exp(-values))
    return gate * (1.0 + values * (1.0 - gate))


def kernel(
    sizes,
    len_ref,
    cot_ref,
    hid_ref,
    lat_ref,
    w_two,
    w_one,
    out_ref,
    wv_two,
    wv_one,
    tmp,
    tmp_back,
    stage_c,
    stage_h,
    recv_c,
    recv_h,
    cots,
    grads,
    acc,
    slope_h,
    slope_l,
    w_sem,
    c_send,
    c_recv,
    h_send,
    h_recv,
    x_send,
    x_recv,
    ga_send,
    ga_recv,
    gb_send,
    gb_recv,
):
    tms, rws, fd, rd, cols, ch = sizes
    group = tms * rws
    frames = tms * fd
    rows = rws * rd
    pix = frames * rows
    dp = lax.axis_index("dp")
    tm = lax.axis_index("tm")
    rw = lax.axis_index("rows")
    me = tm * rws + rw

    def peer(k):
        d_tm = lax.rem(tm + k // rws, tms)
        d_rw = lax.rem(rw + lax.rem(k, rws), rws)
        return d_tm, d_rw

    barrier = pltpu.get_barrier_semaphore()

    def greet(k, carry):
        d_tm, d_rw = peer(k)
        pl.semaphore_signal(barrier, inc=1, device_id=(dp, d_tm, d_rw), device_id_type=MESH)
        return carry

    lax.fori_loop(1, group, greet, 0)

    weight_copies = []
    for n, (src, dst) in enumerate(((w_two, wv_two), (w_one, wv_one))):
        for at, c in enumerate((1, 0, 2)):
            copy = pltpu.make_async_copy(src.at[:, :, c], dst.at[:, :, c], w_sem.at[n, at])
            copy.start()
            weight_copies.append(copy)

    lanes = out_ref.shape[1]
    strips = ch // lanes
    row_of = lax.broadcasted_iota(jnp.int32, (fd * rd, lanes), 0)
    live = tm * fd + row_of // rd < len_ref[0]

    def columns_of(src_ref, dst_ref, at, masked):
        for j in range(strips):
            tmp[j] = src_ref[:, j * lanes : (j + 1) * lanes].astype(F32)

        def one(w, carry):
            for j in range(strips):
                block = tmp.at[j][pl.ds(w, fd * rd, stride=cols), :]
                if masked:
                    block = jnp.where(live, block, 0.0)
                dst_ref[w, at : at + fd * rd, j * lanes : (j + 1) * lanes] = block.astype(BF16)
            return carry

        lax.fori_loop(0, cols, one, 0)

    def send_all(stage, recv, send_sem, recv_sem):
        def one(k, carry):
            d_tm, d_rw = peer(k)
            pltpu.make_async_remote_copy(
                src_ref=stage.at[d_tm * rws + d_rw],
                dst_ref=recv.at[me],
                send_sem=send_sem,
                recv_sem=recv_sem,
                device_id=(dp, d_tm, d_rw),
                device_id_type=MESH,
            ).start()
            return carry

        lax.fori_loop(1, group, one, 0)

    def wait_all(recv, sem):
        part = recv.at[pl.ds(0, group - 1)]
        pltpu.make_async_copy(part, part, sem).wait()

    columns_of(cot_ref, stage_c, 0, True)
    pl.semaphore_wait(barrier, group - 1)
    send_all(stage_c, recv_c, c_send, c_recv)
    columns_of(hid_ref, stage_h, 0, False)
    columns_of(lat_ref, stage_h, fd * rd, False)
    send_all(stage_h, recv_h, h_send, h_recv)
    recv_c[pl.ds(me, 1)] = stage_c[pl.ds(me, 1)]
    recv_h[pl.ds(me, 1)] = stage_h[pl.ds(me, 1)]

    tail = cots.shape[1] - pix
    for buf in (cots, grads):
        buf[:, pl.ds(pix, tail), :] = jnp.zeros((3, tail, ch), BF16)

        @pl.when(me == 0)
        def _():
            buf[2, pl.ds(0, pix), :] = jnp.zeros((pix, ch), BF16)

        @pl.when(me == group - 1)
        def _():
            buf[0, pl.ds(0, pix), :] = jnp.zeros((pix, ch), BF16)

    def gather_rows(recv, at):
        for t in range(tms):
            for pair in range(rws // 2):
                one = recv[t * rws + 2 * pair, at : at + fd * rd, :].astype(F32)
                two = recv[t * rws + 2 * pair + 1, at : at + fd * rd, :].astype(F32)
                for f in range(fd):
                    joined = jnp.concatenate([one[f * rd : (f + 1) * rd], two[f * rd : (f + 1) * rd]], axis=0)
                    start = (t * fd + f) * rows + 2 * pair * rd
                    tmp_back[start : start + 2 * rd, :] = joined

    def to_neighbours(buf, chans, send_sem, recv_sem):
        copies = []
        for to, has, slot in ((me + 1, me < group - 1, 2), (me - 1, me > 0, 0)):
            to = lax.rem(to + group, group)
            copies.append((
                has,
                pltpu.make_async_remote_copy(
                    src_ref=buf.at[1, pl.ds(0, pix), chans],
                    dst_ref=buf.at[slot, pl.ds(0, pix), chans],
                    send_sem=send_sem.at[slot],
                    recv_sem=recv_sem.at[slot],
                    device_id=(dp, to // rws, lax.rem(to, rws)),
                    device_id_type=MESH,
                ),
            ))
        for has, copy in copies:
            pl.when(has)(copy.start)
        return copies

    def wait_recv(copies):
        pl.when(me > 0)(copies[0][1].wait_recv)
        pl.when(me < group - 1)(copies[1][1].wait_recv)

    def wait_send(copies):
        for has, copy in copies:
            pl.when(has)(copy.wait_send)

    wait_all(recv_c, c_recv)
    gather_rows(recv_c, 0)
    cots[1, pl.ds(0, pix), :] = tmp_back[...].astype(BF16)
    x_copies = to_neighbours(cots, pl.ds(0, ch), x_send, x_recv)

    def stacked(buf, columns, ins):
        parts = [buf[c, (2 - a) * rows : (2 - a) * rows + pix, ins] for c in columns for a in range(3)]
        return jnp.concatenate(parts, axis=1)

    def weights(wv, columns, outs, ins):
        return jnp.concatenate(
            [
                jnp.concatenate([wv[a, r, c, outs, ins] for c in columns for a in range(3)], axis=1)
                for r in range(3)
            ],
            axis=0,
        )

    def product(buf, wv, columns, outs, ins):
        return lax.dot_general(
            stacked(buf, columns, ins), weights(wv, columns, outs, ins), NT, preferred_element_type=F32
        )

    every = slice(0, ch)

    def row_taps(above, same, below):
        at_row = lax.rem(lax.broadcasted_iota(jnp.int32, above.shape, 0), rows)
        up = jnp.where(at_row == rows - 1, 0.0, pltpu.roll(above, pix - 1, 0))
        down = jnp.where(at_row == 0, 0.0, pltpu.roll(below, 1, 0))
        return same + up + down

    weight_copies[0].wait()
    acc[...] = product(cots, wv_two, (1,), every, every)

    wait_all(recv_h, h_recv)
    gather_rows(recv_h, 0)
    slope_h[...] = silu_slope(tmp_back[...])
    gather_rows(recv_h, fd * rd)
    slope_l[...] = silu_slope(tmp_back[...])

    weight_copies[1].wait()
    weight_copies[2].wait()
    wait_recv(x_copies)
    g_copies = []
    for outs, send_sem, recv_sem in ((slice(0, SPLIT), ga_send, ga_recv), (slice(SPLIT, ch), gb_send, gb_recv)):
        part = product(cots, wv_two, (0, 2), outs, every)
        n = outs.stop - outs.start
        taps = [
            acc[:, r * ch + outs.start : r * ch + outs.stop] + part[:, r * n : (r + 1) * n] for r in range(3)
        ]
        grads[1, pl.ds(0, pix), outs] = (row_taps(*taps) * slope_h[:, outs]).astype(BF16)
        g_copies.append(to_neighbours(grads, pl.ds(outs.start, n), send_sem, recv_sem))

    weight_copies[3].wait()
    acc[...] = product(grads, wv_one, (1,), every, every)
    weight_copies[4].wait()
    weight_copies[5].wait()
    wait_recv(g_copies[0])
    acc[...] += product(grads, wv_one, (0, 2), every, slice(0, SPLIT))
    wait_recv(g_copies[1])
    part = product(grads, wv_one, (0, 2), every, slice(SPLIT, ch))
    taps = [acc[:, r * ch : (r + 1) * ch] + part[:, r * ch : (r + 1) * ch] for r in range(3)]
    result = cots[1, pl.ds(0, pix), :].astype(F32) + row_taps(*taps) * slope_l[...]
    for j in range(strips):
        out_ref[pl.ds(j, pix, stride=strips), :] = result[:, j * lanes : (j + 1) * lanes]

    wait_all(recv_c, c_send)
    wait_all(recv_h, h_send)
    wait_send(x_copies)
    wait_send(g_copies[0])
    wait_send(g_copies[1])


def on_device(tms, rws, latents, hidden, cotangent, conv_one, conv_two, lengths):
    _, fd, rd, cols, ch = latents.shape
    frames, rows = tms * fd, rws * rd
    pix = frames * rows
    local = fd * rd * cols
    group = tms * rws
    flat = lambda x: x.reshape(local, ch)
    vmem = pl.BlockSpec(memory_space=pltpu.VMEM)
    hbm = pl.BlockSpec(memory_space=pltpu.HBM)
    dma = pltpu.SemaphoreType.DMA
    out = pl.pallas_call(
        functools.partial(kernel, (tms, rws, fd, rd, cols, ch)),
        out_shape=jax.ShapeDtypeStruct((pix * ch // 128, 128), F32),
        in_specs=[pl.BlockSpec(memory_space=pltpu.SMEM), vmem, vmem, vmem, hbm, hbm],
        out_specs=vmem,
        scratch_shapes=[
            pltpu.VMEM(conv_two.shape, BF16),
            pltpu.VMEM(conv_one.shape, BF16),
            pltpu.VMEM((ch // 128, local, 128), F32),
            pltpu.VMEM((pix, ch), F32),
            pltpu.VMEM((group, fd * rd, ch), BF16),
            pltpu.VMEM((group, 2 * fd * rd, ch), BF16),
            pltpu.VMEM((group, fd * rd, ch), BF16),
            pltpu.VMEM((group, 2 * fd * rd, ch), BF16),
            pltpu.VMEM((3, pix + 2 * rows, ch), BF16),
            pltpu.VMEM((3, pix + 2 * rows, ch), BF16),
            pltpu.VMEM((pix, 3 * ch), F32),
            pltpu.VMEM((pix, ch), F32),
            pltpu.VMEM((pix, ch), F32),
            dma((2, 3)),
            dma,
            dma,
            dma,
            dma,
            dma((3,)),
            dma((3,)),
            dma((3,)),
            dma((3,)),
            dma((3,)),
            dma((3,)),
        ],
        compiler_params=pltpu.CompilerParams(
            collective_id=0, has_side_effects=True, vmem_limit_bytes=56 * 1024 * 1024
        ),
        name="column_block",
    )(lengths, flat(cotangent), flat(hidden), flat(latents), conv_two, conv_one)
    return out.reshape(1, frames, rows, 1, ch)


def solution(mesh):
    in_specs = (
        P("dp", "tm", "rows", None, None),
        P("dp", "tm", "rows", None, None),
        P("dp", "tm", "rows", None, None),
        P(),
        P(),
        P("dp"),
    )
    out_specs = P("dp", None, None, ("tm", "rows"), None)
    return jax.shard_map(
        functools.partial(on_device, mesh.shape["tm"], mesh.shape["rows"]),
        mesh=mesh,
        in_specs=in_specs,
        out_specs=out_specs,
        check_vma=False,
    )
```

time: 111 us -> 30.9 us (0.28)
  local copies, waits for them, and re-layouts: 39 us -> 2.01 us
  Pallas kernels: 0 us -> 27.8 us
  blocking collectives: 25.5 us -> 0 us
  starting transfers between devices: 18.2 us -> 0 us
  waiting for transfers between devices: 10.3 us -> 0 us
  matrix products: 10.2 us -> 0 us
  other arithmetic: 5.43 us -> 0 us
    pallas_call x0 -> x1, Pallas kernels: none -> 27.8 us  [on_device(): pl.pallas_call(functools.partial(kernel, (tms, rws, fd, rd, cols, ch)), o...]
    rev x18 -> x0, local copies, waits for them, and re-layouts: 26.5 us -> none  [transposed_conv(): kernel_slice = kernel[2 - time_tap, 2 - row_tap, ::-1]]
    all_to_all x2 -> x0, blocking collectives: 25.5 us -> none  [the longest x1 13.1 us: on_device(): lax.all_to_all(lax.all_to_all(result, 'tm', split_axis=3, concat_axis=1,...]
    ppermute x6 -> x0, starting transfers between devices: 18.2 us -> none  [the longest x2 11.4 us: with_halo(): lax.ppermute(lax.slice_in_dim(block, block.shape[dim] - width, None, axis...]
    ppermute x6 -> x0, waiting for transfers between devices: 10.3 us -> none  [the longest x2 6.78 us: shifted(): return lax.ppermute(value, axis, pairs)]
    dot_general x18 -> x0, matrix products: 10.2 us -> none  [transposed_conv(): jnp.einsum('frwkc,kdc->frwd', stacked, kernel_slice, preferred_element_ty...]
    slice x4 -> x0, local copies, waits for them, and re-layouts: 8.07 us -> none  [the longest x2 8.04 us: transposed_conv(): kernel_slice = kernel[2 - time_tap, 2 - row_tap, ::-1]]
    another operation x6 -> x0, local copies, waits for them, and re-layouts: 2.65 us -> none  [transposed_conv(): jnp.stack([slab_rows[:, :, col_tap:col_tap + col_count] for col_tap in ra...]
  transfers between devices with their start and end apart: 6 -> 0, of which waited for: 2 -> 0; matrix products, arithmetic and copies ran while one was open for 33% -> 0% of each run, Pallas kernels for 0% -> 0%
where the time goes in v1:
time: 30.9 us; the launch traced here: 30.4 us
  Pallas kernels  27.8 us (90%)
  local copies, waits for them, and re-layouts  2.01 us (7%)
  between operations  0.66 us (2%)
    pallas_call x1, Pallas kernels, on_device(): pl.pallas_call(functools.partial(kernel, (tms, rws, fd, rd, cols, ch)), o...  27.8 us
    unnamed x1, local copies, waits for them, and re-layouts  2.01 us

profile of v1, /device:TPU:1, one launch (start us, length us, event | category | flops | bytes accessed | tf_op | source)
XLA Modules:
  0.0 30.4 jit_solution(17360175843641776969)
XLA Ops:
  0.7 27.8 %column_block.1 = f32[768,128]{1,0:T(8,128)} custom-call(s32[1]{0:T(128)S(6)} %copy.9.len_ref, bf16[256,384]{1,0:T(8,128)(2,1)} %bitcast.5, bf16[256,384]{1,0:T(8,128)(2,1)} %bitcast.6, bf16[256,384]{1,0:T(8,128)(2,1)} %bitcast.7, bf16[3,3,3,384,384]{4,3,2,1,0:T(8,128)(2,1)} %w_two.1, bf16[3,3,3,384,384]{4,3,2,1,0:T(8,128)(2,1)} %w_one.1), custom_call_target="tpu_custom_call" | custom-call | tf_op jit(solution)/shard_map/column_block/pallas_call | solution.py:266
  28.4 2.0 %copy.10 = f32[1,8,32,1,384]{4,3,2,1,0:T(1,128)} copy(f32[1,8,32,1,384]{4,3,2,1,0:T(1,128)} %bitcast.4) | data formatting | bytes 786432

commit v2 on v1

--- a/solution.py
+++ b/solution.py
@@ -30,22 +30,30 @@
     out_ref,
     wv_two,
     wv_one,
+    cot_in,
+    hid_in,
+    lat_in,
     tmp,
     tmp_back,
     stage_c,
     stage_h,
+    stage_l,
     recv_c,
     recv_h,
+    recv_l,
     cots,
     grads,
     acc,
     slope_h,
     slope_l,
+    in_sem,
     w_sem,
     c_send,
     c_recv,
     h_send,
     h_recv,
+    l_send,
+    l_recv,
     x_send,
     x_recv,
     ga_send,
@@ -63,20 +71,30 @@
     rw = lax.axis_index("rows")
     me = tm * rws + rw
 
-    def peer(k):
-        d_tm = lax.rem(tm + k // rws, tms)
-        d_rw = lax.rem(rw + lax.rem(k, rws), rws)
-        return d_tm, d_rw
+    def each_peer(action):
+        for step in sorted(range(tms), key=lambda s: -min(s, tms - s)):
+
+            def one(k, carry, step=step):
+                turn = k if step == 0 else lax.rem(k + rws // 2 - 1, rws)
+                action(lax.rem(tm + step, tms), lax.rem(rw + turn, rws))
+                return carry
+
+            lax.fori_loop(1 if step == 0 else 0, rws, one, 0)
+
+    own_copies = []
+    for n, (src, dst) in enumerate(((cot_ref, cot_in), (hid_ref, hid_in), (lat_ref, lat_in))):
+        own_copies.append(pltpu.make_async_copy(src, dst, in_sem.at[n]))
+    own_copies[0].start()
 
     barrier = pltpu.get_barrier_semaphore()
-
-    def greet(k, carry):
-        d_tm, d_rw = peer(k)
-        pl.semaphore_signal(barrier, inc=1, device_id=(dp, d_tm, d_rw), device_id_type=MESH)
-        return carry
-
-    lax.fori_loop(1, group, greet, 0)
-
+    each_peer(
+        lambda d_tm, d_rw: pl.semaphore_signal(
+            barrier, inc=1, device_id=(dp, d_tm, d_rw), device_id_type=MESH
+        )
+    )
+
+    own_copies[1].start()
+    own_copies[2].start()
     weight_copies = []
     for n, (src, dst) in enumerate(((w_two, wv_two), (w_one, wv_one))):
         for at, c in enumerate((1, 0, 2)):
@@ -89,7 +107,7 @@
     row_of = lax.broadcasted_iota(jnp.int32, (fd * rd, lanes), 0)
     live = tm * fd + row_of // rd < len_ref[0]
 
-    def columns_of(src_ref, dst_ref, at, masked):
+    def columns_of(src_ref, dst_ref, masked):
         for j in range(strips):
             tmp[j] = src_ref[:, j * lanes : (j + 1) * lanes].astype(F32)
 
@@ -98,15 +116,14 @@
                 block = tmp.at[j][pl.ds(w, fd * rd, stride=cols), :]
                 if masked:
                     block = jnp.where(live, block, 0.0)
-                dst_ref[w, at : at + fd * rd, j * lanes : (j + 1) * lanes] = block.astype(BF16)
+                dst_ref[w, :, j * lanes : (j + 1) * lanes] = block.astype(BF16)
             return carry
 
         lax.fori_loop(0, cols, one, 0)
 
     def send_all(stage, recv, send_sem, recv_sem):
-        def one(k, carry):
-            d_tm, d_rw = peer(k)
-            pltpu.make_async_remote_copy(
+        each_peer(
+            lambda d_tm, d_rw: pltpu.make_async_remote_copy(
                 src_ref=stage.at[d_tm * rws + d_rw],
                 dst_ref=recv.at[me],
                 send_sem=send_sem,
@@ -114,22 +131,24 @@
                 device_id=(dp, d_tm, d_rw),
                 device_id_type=MESH,
             ).start()
-            return carry
-
-        lax.fori_loop(1, group, one, 0)
+        )
 
     def wait_all(recv, sem):
         part = recv.at[pl.ds(0, group - 1)]
         pltpu.make_async_copy(part, part, sem).wait()
 
-    columns_of(cot_ref, stage_c, 0, True)
+    own_copies[0].wait()
+    columns_of(cot_in, stage_c, True)
     pl.semaphore_wait(barrier, group - 1)
     send_all(stage_c, recv_c, c_send, c_recv)
-    columns_of(hid_ref, stage_h, 0, False)
-    columns_of(lat_ref, stage_h, fd * rd, False)
+    own_copies[1].wait()
+    columns_of(hid_in, stage_h, False)
     send_all(stage_h, recv_h, h_send, h_recv)
+    own_copies[2].wait()
+    columns_of(lat_in, stage_l, False)
     recv_c[pl.ds(me, 1)] = stage_c[pl.ds(me, 1)]
     recv_h[pl.ds(me, 1)] = stage_h[pl.ds(me, 1)]
+    recv_l[pl.ds(me, 1)] = stage_l[pl.ds(me, 1)]
 
     tail = cots.shape[1] - pix
     for buf in (cots, grads):
@@ -143,11 +162,11 @@
         def _():
             buf[0, pl.ds(0, pix), :] = jnp.zeros((pix, ch), BF16)
 
-    def gather_rows(recv, at):
+    def gather_rows(recv):
         for t in range(tms):
             for pair in range(rws // 2):
-                one = recv[t * rws + 2 * pair, at : at + fd * rd, :].astype(F32)
-                two = recv[t * rws + 2 * pair + 1, at : at + fd * rd, :].astype(F32)
+                one = recv[t * rws + 2 * pair].astype(F32)
+                two = recv[t * rws + 2 * pair + 1].astype(F32)
                 for f in range(fd):
                     joined = jnp.concatenate([one[f * rd : (f + 1) * rd], two[f * rd : (f + 1) * rd]], axis=0)
                     start = (t * fd + f) * rows + 2 * pair * rd
@@ -181,7 +200,7 @@
             pl.when(has)(copy.wait_send)
 
     wait_all(recv_c, c_recv)
-    gather_rows(recv_c, 0)
+    gather_rows(recv_c)
     cots[1, pl.ds(0, pix), :] = tmp_back[...].astype(BF16)
     x_copies = to_neighbours(cots, pl.ds(0, ch), x_send, x_recv)
 
@@ -213,12 +232,11 @@
 
     weight_copies[0].wait()
     acc[...] = product(cots, wv_two, (1,), every, every)
+    send_all(stage_l, recv_l, l_send, l_recv)
 
     wait_all(recv_h, h_recv)
-    gather_rows(recv_h, 0)
+    gather_rows(recv_h)
     slope_h[...] = silu_slope(tmp_back[...])
-    gather_rows(recv_h, fd * rd)
-    slope_l[...] = silu_slope(tmp_back[...])
 
     weight_copies[1].wait()
     weight_copies[2].wait()
@@ -235,6 +253,9 @@
 
     weight_copies[3].wait()
     acc[...] = product(grads, wv_one, (1,), every, every)
+    wait_all(recv_l, l_recv)
+    gather_rows(recv_l)
+    slope_l[...] = silu_slope(tmp_back[...])
     weight_copies[4].wait()
     weight_copies[5].wait()
     wait_recv(g_copies[0])
@@ -248,9 +269,16 @@
 
     wait_all(recv_c, c_send)
     wait_all(recv_h, h_send)
+    wait_all(recv_l, l_send)
     wait_send(x_copies)
     wait_send(g_copies[0])
     wait_send(g_copies[1])
+
+
+def settle(src_ref, dst_ref, sem):
+    copy = pltpu.make_async_copy(src_ref, dst_ref, sem)
+    copy.start()
+    copy.wait()
 
 
 def on_device(tms, rws, latents, hidden, cotangent, conv_one, conv_two, lengths):
@@ -266,39 +294,38 @@
     out = pl.pallas_call(
         functools.partial(kernel, (tms, rws, fd, rd, cols, ch)),
         out_shape=jax.ShapeDtypeStruct((pix * ch // 128, 128), F32),
-        in_specs=[pl.BlockSpec(memory_space=pltpu.SMEM), vmem, vmem, vmem, hbm, hbm],
+        in_specs=[pl.BlockSpec(memory_space=pltpu.SMEM), *[hbm] * 5],
         out_specs=vmem,
         scratch_shapes=[
             pltpu.VMEM(conv_two.shape, BF16),
             pltpu.VMEM(conv_one.shape, BF16),
+            *[pltpu.VMEM((local, ch), BF16)] * 3,
             pltpu.VMEM((ch // 128, local, 128), F32),
             pltpu.VMEM((pix, ch), F32),
-            pltpu.VMEM((group, fd * rd, ch), BF16),
-            pltpu.VMEM((group, 2 * fd * rd, ch), BF16),
-            pltpu.VMEM((group, fd * rd, ch), BF16),
-            pltpu.VMEM((group, 2 * fd * rd, ch), BF16),
+            *[pltpu.VMEM((group, fd * rd, ch), BF16)] * 6,
             pltpu.VMEM((3, pix + 2 * rows, ch), BF16),
             pltpu.VMEM((3, pix + 2 * rows, ch), BF16),
             pltpu.VMEM((pix, 3 * ch), F32),
             pltpu.VMEM((pix, ch), F32),
             pltpu.VMEM((pix, ch), F32),
+            dma((3,)),
             dma((2, 3)),
-            dma,
-            dma,
-            dma,
-            dma,
-            dma((3,)),
-            dma((3,)),
-            dma((3,)),
-            dma((3,)),
-            dma((3,)),
-            dma((3,)),
+            *[dma] * 6,
+            *[dma((3,))] * 6,
         ],
         compiler_params=pltpu.CompilerParams(
             collective_id=0, has_side_effects=True, vmem_limit_bytes=56 * 1024 * 1024
         ),
         name="column_block",
     )(lengths, flat(cotangent), flat(hidden), flat(latents), conv_two, conv_one)
+    out = pl.pallas_call(
+        settle,
+        out_shape=jax.ShapeDtypeStruct(out.shape, F32),
+        in_specs=[pl.BlockSpec(memory_space=pl.ANY)],
+        out_specs=pl.BlockSpec(memory_space=pl.ANY),
+        scratch_shapes=[dma],
+        name="settle",
+    )(out)
     return out.reshape(1, frames, rows, 1, ch)
 
 

time: 30.9 us -> 40.8 us (1.32)
  Pallas kernels: 27.8 us -> 39.8 us
  local copies, waits for them, and re-layouts: 2.01 us -> 0 us
    pallas_call x0 -> x1, Pallas kernels: none -> 13 us  [on_device(): pl.pallas_call(settle, out_shape=jax.ShapeDtypeStruct(out.shape, F32), in...]
    unnamed x1 -> x0, local copies, waits for them, and re-layouts: 2.01 us -> none
    pallas_call x1, Pallas kernels: 27.8 us -> 26.8 us  [on_device(): pl.pallas_call(functools.partial(kernel, (tms, rws, fd, rd, cols, ch)), o...]
where the time goes in v2:
time: 40.8 us; the launch traced here: 40.4 us
  Pallas kernels  39.8 us (98%)
  between operations  0.66 us (2%)
    pallas_call x1, Pallas kernels, on_device(): pl.pallas_call(functools.partial(kernel, (tms, rws, fd, rd, cols, ch)), o...  26.8 us
    pallas_call x1, Pallas kernels, on_device(): pl.pallas_call(settle, out_shape=jax.ShapeDtypeStruct(out.shape, F32), in...  13 us

profile of v2, /device:TPU:1, one launch (start us, length us, event | category | flops | bytes accessed | tf_op | source)
XLA Modules:
  0.0 40.4 jit_solution(9312192492075587093)
XLA Ops:
  0.7 26.8 %column_block.1.src_ref = f32[768,128]{1,0:T(8,128)} custom-call(s32[1]{0:T(128)S(6)} %copy.8.len_ref, bf16[256,384]{1,0:T(8,128)(2,1)} %bitcast.4, bf16[256,384]{1,0:T(8,128)(2,1)} %bitcast.5, bf16[256,384]{1,0:T(8,128)(2,1)} %bitcast.6, bf16[3,3,3,384,384]{4,3,2,1,0:T(8,128)(2,1)} %w_two.1, bf16[3,3,3,384,384]{4,3,2,1,0:T(8,128)(2,1)} %w_one.1), custom_call_target="tpu_custom_call" | custom-call | tf_op jit(solution)/shard_map/column_block/pallas_call | solution.py:294
  27.4 13.0 %settle.1 = f32[768,128]{1,0:T(8,128)} custom-call(f32[768,128]{1,0:T(8,128)} %column_block.1.src_ref), custom_call_target="tpu_custom_call" | custom-call | tf_op jit(solution)/shard_map/settle/pallas_call | solution.py:321

commit v3 on v2

v3 whole, which is shorter than its diff:
```python
import functools

import jax
import jax.numpy as jnp
from jax import lax
from jax.experimental import pallas as pl
from jax.experimental.pallas import tpu as pltpu
from jax.sharding import PartitionSpec as P

MESH = pl.DeviceIdType.MESH
NT = (((1,), (1,)), ((), ()))
F32 = jnp.float32
BF16 = jnp.bfloat16
SPLIT = 256


def silu_slope(values):
    gate = 1.0 / (1.0 + jnp.exp(-values))
    return gate * (1.0 + values * (1.0 - gate))


def kernel(
    sizes,
    len_ref,
    cot_ref,
    hid_ref,
    lat_ref,
    w_two,
    w_one,
    out_ref,
    masked_out,
    wv_two,
    wv_one,
    cot_in,
    hid_in,
    lat_in,
    tmp,
    tmp_back,
    stage_c,
    stage_h,
    stage_l,
    recv_c,
    recv_h,
    recv_l,
    cots,
    grads,
    acc,
    slope_h,
    slope_l,
    in_sem,
    w_sem,
    c_send,
    c_recv,
    h_send,
    h_recv,
    l_send,
    l_recv,
    x_sem,
    g_sem,
):
    tms, rws, fd, rd, cols, ch = sizes
    group = tms * rws
    frames = tms * fd
    rows = rws * rd
    pix = frames * rows
    dp = lax.axis_index("dp")
    tm = lax.axis_index("tm")
    rw = lax.axis_index("rows")
    me = tm * rws + rw
    odd = lax.rem(rw, 2)
    mate_slot = 2 * odd
    outer_slot = 2 - 2 * odd

    def each_peer(action):
        for step in sorted(range(tms), key=lambda s: -min(s, tms - s)):

            def one(k, carry, step=step):
                turn = k if step == 0 else lax.rem(k + rws // 2 - 1, rws)
                action(lax.rem(tm + step, tms), lax.rem(rw + turn, rws))
                return carry

            lax.fori_loop(1 if step == 0 else 0, rws, one, 0)

    own_copies = []
    for n, (src, dst) in enumerate(((cot_ref, cot_in), (hid_ref, hid_in), (lat_ref, lat_in))):
        own_copies.append(pltpu.make_async_copy(src, dst, in_sem.at[n]))
    own_copies[0].start()

    barrier = pltpu.get_barrier_semaphore()
    each_peer(
        lambda d_tm, d_rw: pl.semaphore_signal(
            barrier, inc=1, device_id=(dp, d_tm, d_rw), device_id_type=MESH
        )
    )

    own_copies[1].start()
    own_copies[2].start()
    weight_copies = []
    for n, (src, dst) in enumerate(((w_two, wv_two), (w_one, wv_one))):
        for at, c in enumerate((1, 0, 2)):
            copy = pltpu.make_async_copy(src.at[:, :, c], dst.at[:, :, c], w_sem.at[n, at])
            copy.start()
            weight_copies.append(copy)

    lanes = out_ref.shape[1]
    strips = ch // lanes
    row_of = lax.broadcasted_iota(jnp.int32, (fd * rd, lanes), 0)
    live = tm * fd + row_of // rd < len_ref[0]

    def columns_of(src_ref, dst_ref, first, masked):
        for j in range(strips):
            tmp[j] = src_ref[:, j * lanes : (j + 1) * lanes].astype(F32)

        def one(w, carry):
            for j in range(strips):
                block = tmp.at[j][pl.ds(w, fd * rd, stride=cols), :]
                if masked:
                    block = jnp.where(live, block, 0.0)
                dst_ref[first + w, :, j * lanes : (j + 1) * lanes] = block.astype(BF16)
            return carry

        lax.fori_loop(0, cols, one, 0)

    def pair_at(device):
        return pl.ds(device + lax.rem(device, 2), 2)

    def send_all(stage, recv, at, send_sem, recv_sem):
        each_peer(
            lambda d_tm, d_rw: pltpu.make_async_remote_copy(
                src_ref=stage.at[at(d_tm * rws + d_rw)],
                dst_ref=recv.at[me],
                send_sem=send_sem,
                recv_sem=recv_sem,
                device_id=(dp, d_tm, d_rw),
                device_id_type=MESH,
            ).start()
        )

    def wait_all(recv, sem):
        part = recv.at[pl.ds(0, group - 1)]
        pltpu.make_async_copy(part, part, sem).wait()

    no_column = jnp.zeros((fd * rd, ch), BF16)
    stage_c[0] = no_column
    stage_c[cols + 1] = no_column
    own_copies[0].wait()
    columns_of(cot_in, stage_c, 1, True)
    pl.semaphore_wait(barrier, group - 1)
    send_all(stage_c, recv_c, pair_at, c_send, c_recv)
    own_copies[1].wait()
    columns_of(hid_in, stage_h, 0, False)
    send_all(stage_h, recv_h, lambda device: device, h_send, h_recv)
    own_copies[2].wait()
    columns_of(lat_in, stage_l, 0, False)
    send_all(stage_l, recv_l, lambda device: device, l_send, l_recv)
    recv_c[me] = stage_c[pair_at(me)]
    recv_h[me] = stage_h[me]
    recv_l[me] = stage_l[me]

    tail = cots.shape[1] - pix
    for buf in (cots, grads):
        buf[:, pl.ds(pix, tail), :] = jnp.zeros((3, tail, ch), BF16)

    @pl.when((me == 0) | (me == group - 1))
    def _():
        grads[outer_slot, pl.ds(0, pix), :] = jnp.zeros((pix, ch), BF16)

    def gather_rows(block):
        for t in range(tms):
            for pair in range(rws // 2):
                one = block(t * rws + 2 * pair).astype(F32)
                two = block(t * rws + 2 * pair + 1).astype(F32)
                for f in range(fd):
                    joined = jnp.concatenate([one[f * rd : (f + 1) * rd], two[f * rd : (f + 1) * rd]], axis=0)
                    start = (t * fd + f) * rows + 2 * pair * rd
                    tmp_back[start : start + 2 * rd, :] = joined

    def copy_column(buf, chans, slot, target, send_sem, recv_sem):
        return pltpu.make_async_remote_copy(
            src_ref=buf.at[1, pl.ds(0, pix), chans],
            dst_ref=buf.at[slot, pl.ds(0, pix), chans],
            send_sem=send_sem,
            recv_sem=recv_sem,
            device_id=(dp, target // rws, lax.rem(target, rws)),
            device_id_type=MESH,
        )

    def to_mate(buf, chans, sems):
        return copy_column(buf, chans, outer_slot, me + 1 - 2 * odd, *sems)

    inner = (me > 0) & (me < group - 1)

    def to_outer(buf, chans, sems):
        return copy_column(buf, chans, mate_slot, lax.rem(me + 2 * odd - 1 + group, group), *sems)

    wait_all(recv_c, c_recv)
    gather_rows(lambda source: recv_c[source, 1 - odd])
    cots[1, pl.ds(0, pix), :] = tmp_back[...].astype(BF16)
    mate_copy = to_mate(cots, pl.ds(0, ch), (x_sem.at[0], x_sem.at[1]))
    mate_copy.start()
    gather_rows(lambda source: recv_c[source, odd])
    cots[outer_slot, pl.ds(0, pix), :] = tmp_back[...].astype(BF16)

    def stacked(buf, columns, ins):
        parts = [buf[c, (2 - a) * rows : (2 - a) * rows + pix, ins] for c in columns for a in range(3)]
        return jnp.concatenate(parts, axis=1)

    def weights(wv, columns, outs, ins):
        return jnp.concatenate(
            [
                jnp.concatenate([wv[a, r, c, outs, ins] for c in columns for a in range(3)], axis=1)
                for r in range(3)
            ],
            axis=0,
        )

    def product(buf, wv, columns, outs, ins):
        return lax.dot_general(
            stacked(buf, columns, ins), weights(wv, columns, outs, ins), NT, preferred_element_type=F32
        )

    every = slice(0, ch)

    def row_taps(above, same, below):
        at_row = lax.rem(lax.broadcasted_iota(jnp.int32, above.shape, 0), rows)
        up = jnp.where(at_row == rows - 1, 0.0, pltpu.roll(above, pix - 1, 0))
        down = jnp.where(at_row == 0, 0.0, pltpu.roll(below, 1, 0))
        return same + up + down

    for copy in weight_copies[:3]:
        copy.wait()
    g_copies = []
    for at, outs in enumerate((slice(0, SPLIT), slice(SPLIT, ch))):
        n = outs.stop - outs.start
        acc[:, : 3 * n] = product(cots, wv_two, (1, outer_slot), outs, every)
        if at == 0:
            wait_all(recv_h, h_recv)
            gather_rows(lambda source: recv_h[source])
            slope_h[...] = silu_slope(tmp_back[...])
            mate_copy.wait_recv()
        part = product(cots, wv_two, (mate_slot,), outs, every)
        taps = [acc[:, r * n : (r + 1) * n] + part[:, r * n : (r + 1) * n] for r in range(3)]
        grads[1, pl.ds(0, pix), outs] = (row_taps(*taps) * slope_h[:, outs]).astype(BF16)
        chans = pl.ds(outs.start, n)
        outer = to_outer(grads, chans, (g_sem.at[at, 0], g_sem.at[at, 1]))
        mate = to_mate(grads, chans, (g_sem.at[at, 2], g_sem.at[at, 3]))
        pl.when(inner)(outer.start)
        mate.start()
        g_copies.append((outer, mate))

    for copy in weight_copies[3:]:
        copy.wait()
    acc[...] = product(grads, wv_one, (1,), every, every)
    masked = cots[1, pl.ds(0, pix), :].astype(F32)
    for j in range(strips):
        masked_out[pl.ds(j, pix, stride=strips), :] = masked[:, j * lanes : (j + 1) * lanes]
    for _, mate in g_copies:
        mate.wait_recv()
    acc[...] += product(grads, wv_one, (mate_slot,), every, every)
    wait_all(recv_l, l_recv)
    gather_rows(lambda source: recv_l[source])
    slope_l[...] = silu_slope(tmp_back[...])
    pl.when(inner)(g_copies[0][0].wait_recv)
    acc[...] += product(grads, wv_one, (outer_slot,), every, slice(0, SPLIT))
    pl.when(inner)(g_copies[1][0].wait_recv)
    part = product(grads, wv_one, (outer_slot,), every, slice(SPLIT, ch))
    taps = [acc[:, r * ch : (r + 1) * ch] + part[:, r * ch : (r + 1) * ch] for r in range(3)]
    result = row_taps(*taps) * slope_l[...]
    for j in range(strips):
        out_ref[pl.ds(j, pix, stride=strips), :] = result[:, j * lanes : (j + 1) * lanes]

    wait_all(recv_c, c_send)
    wait_all(recv_h, h_send)
    wait_all(recv_l, l_send)
    mate_copy.wait_send()
    for outer, mate in g_copies:
        pl.when(inner)(outer.wait_send)
        mate.wait_send()


def on_device(tms, rws, latents, hidden, cotangent, conv_one, conv_two, lengths):
    _, fd, rd, cols, ch = latents.shape
    frames, rows = tms * fd, rws * rd
    pix = frames * rows
    local = fd * rd * cols
    group = tms * rws
    flat = lambda x: x.reshape(local, ch)
    vmem = pl.BlockSpec(memory_space=pltpu.VMEM)
    hbm = pl.BlockSpec(memory_space=pltpu.HBM)
    dma = pltpu.SemaphoreType.DMA
    out, masked = pl.pallas_call(
        functools.partial(kernel, (tms, rws, fd, rd, cols, ch)),
        out_shape=[jax.ShapeDtypeStruct((pix * ch // 128, 128), F32)] * 2,
        in_specs=[pl.BlockSpec(memory_space=pltpu.SMEM), *[hbm] * 5],
        out_specs=[vmem, vmem],
        scratch_shapes=[
            pltpu.VMEM(conv_two.shape, BF16),
            pltpu.VMEM(conv_one.shape, BF16),
            *[pltpu.VMEM((local, ch), BF16)] * 3,
            pltpu.VMEM((ch // 128, local, 128), F32),
            pltpu.VMEM((pix, ch), F32),
            pltpu.VMEM((cols + 2, fd * rd, ch), BF16),
            *[pltpu.VMEM((cols, fd * rd, ch), BF16)] * 2,
            pltpu.VMEM((group, 2, fd * rd, ch), BF16),
            *[pltpu.VMEM((group, fd * rd, ch), BF16)] * 2,
            pltpu.VMEM((3, pix + 2 * rows, ch), BF16),
            pltpu.VMEM((3, pix + 2 * rows, ch), BF16),
            pltpu.VMEM((pix, 3 * ch), F32),
            pltpu.VMEM((pix, ch), F32),
            pltpu.VMEM((pix, ch), F32),
            dma((3,)),
            dma((2, 3)),
            *[dma] * 6,
            dma((2,)),
            dma((2, 4)),
        ],
        compiler_params=pltpu.CompilerParams(
            collective_id=0, has_side_effects=True, vmem_limit_bytes=56 * 1024 * 1024
        ),
        name="column_block",
    )(lengths, flat(cotangent), flat(hidden), flat(latents), conv_two, conv_one)
    out = masked + out
    return out.reshape(1, frames, rows, 1, ch)


def solution(mesh):
    in_specs = (
        P("dp", "tm", "rows", None, None),
        P("dp", "tm", "rows", None, None),
        P("dp", "tm", "rows", None, None),
        P(),
        P(),
        P("dp"),
    )
    out_specs = P("dp", None, None, ("tm", "rows"), None)
    return jax.shard_map(
        functools.partial(on_device, mesh.shape["tm"], mesh.shape["rows"]),
        mesh=mesh,
        in_specs=in_specs,
        out_specs=out_specs,
        check_vma=False,
    )
```

time: 40.8 us -> 28 us (0.69)
  Pallas kernels: 39.8 us -> 25.3 us
  other arithmetic: 0 us -> 1.9 us
    pallas_call x1 -> x0, Pallas kernels: 13 us -> none  [on_device(): pl.pallas_call(settle, out_shape=jax.ShapeDtypeStruct(out.shape, F32), in...]
    add x0 -> x1, other arithmetic: none -> 1.9 us  [on_device(): out = masked + out]
    pallas_call x1, Pallas kernels: 26.8 us -> 25.3 us  [on_device(): pl.pallas_call(functools.partial(kernel, (tms, rws, fd, rd, cols, ch)), o...]
where the time goes in v3:
time: 28 us; the launch traced here: 27.8 us
  Pallas kernels  25.3 us (90%)
  other arithmetic  1.9 us (7%)
  between operations  0.66 us (2%)
    pallas_call x1, Pallas kernels, on_device(): pl.pallas_call(functools.partial(kernel, (tms, rws, fd, rd, cols, ch)), o...  25.3 us
    add x1, other arithmetic, on_device(): out = masked + out  1.9 us

profile of v3, /device:TPU:1, one launch (start us, length us, event | category | flops | bytes accessed | tf_op | source)
XLA Modules:
  0.0 27.8 jit_solution(819395337205158672)
XLA Ops:
  0.7 25.3 %column_block.1 = (f32[768,128]{1,0:T(8,128)}, f32[768,128]{1,0:T(8,128)}) custom-call(s32[1]{0:T(128)S(6)} %copy.8.len_ref, bf16[256,384]{1,0:T(8,128)(2,1)} %bitcast.4, bf16[256,384]{1,0:T(8,128)(2,1)} %bitcast.5, bf16[256,384]{1,0:T(8,128)(2,1)} %bitcast.6, bf16[3,3,3,384,384]{4,3,2,1,0:T(8,128)(2,1)} %w_two.1, bf16[3,3,3,384,384]{4,3,2,1,0:T(8,128)(2,1)} %w_one.1), custom_call_target="tpu_custom_call" | custom-call | tf_op jit(solution)/shard_map/column_block/pallas_call | solution.py:291
  25.9 1.9 %add.3 = f32[768,128]{1,0:T(8,128)} add(f32[768,128]{1,0:T(8,128)} %get-tuple-element.7, f32[768,128]{1,0:T(8,128)} %get-tuple-element.8) | non-fusion elementwise | flops 98304 | bytes 1179648 | tf_op jit(solution)/shard_map/add | solution.py:322

commit v4 on v3

--- a/solution.py
+++ b/solution.py
@@ -28,7 +28,6 @@
     w_two,
     w_one,
     out_ref,
-    masked_out,
     wv_two,
     wv_one,
     cot_in,
@@ -251,9 +250,6 @@
     for copy in weight_copies[3:]:
         copy.wait()
     acc[...] = product(grads, wv_one, (1,), every, every)
-    masked = cots[1, pl.ds(0, pix), :].astype(F32)
-    for j in range(strips):
-        masked_out[pl.ds(j, pix, stride=strips), :] = masked[:, j * lanes : (j + 1) * lanes]
     for _, mate in g_copies:
         mate.wait_recv()
     acc[...] += product(grads, wv_one, (mate_slot,), every, every)
@@ -265,7 +261,7 @@
     pl.when(inner)(g_copies[1][0].wait_recv)
     part = product(grads, wv_one, (outer_slot,), every, slice(SPLIT, ch))
     taps = [acc[:, r * ch : (r + 1) * ch] + part[:, r * ch : (r + 1) * ch] for r in range(3)]
-    result = row_taps(*taps) * slope_l[...]
+    result = cots[1, pl.ds(0, pix), :].astype(F32) + row_taps(*taps) * slope_l[...]
     for j in range(strips):
         out_ref[pl.ds(j, pix, stride=strips), :] = result[:, j * lanes : (j + 1) * lanes]
 
@@ -284,15 +280,16 @@
     pix = frames * rows
     local = fd * rd * cols
     group = tms * rws
-    flat = lambda x: x.reshape(local, ch)
+    in_hbm = lambda x: pltpu.with_memory_space_constraint(x, pltpu.HBM)
+    flat = lambda x: in_hbm(x.reshape(local, ch))
     vmem = pl.BlockSpec(memory_space=pltpu.VMEM)
     hbm = pl.BlockSpec(memory_space=pltpu.HBM)
     dma = pltpu.SemaphoreType.DMA
-    out, masked = pl.pallas_call(
+    out = pl.pallas_call(
         functools.partial(kernel, (tms, rws, fd, rd, cols, ch)),
-        out_shape=[jax.ShapeDtypeStruct((pix * ch // 128, 128), F32)] * 2,
+        out_shape=jax.ShapeDtypeStruct((pix * ch // 128, 128), F32),
         in_specs=[pl.BlockSpec(memory_space=pltpu.SMEM), *[hbm] * 5],
-        out_specs=[vmem, vmem],
+        out_specs=vmem,
         scratch_shapes=[
             pltpu.VMEM(conv_two.shape, BF16),
             pltpu.VMEM(conv_one.shape, BF16),
@@ -315,11 +312,10 @@
             dma((2, 4)),
         ],
         compiler_params=pltpu.CompilerParams(
-            collective_id=0, has_side_effects=True, vmem_limit_bytes=56 * 1024 * 1024
+            collective_id=0, has_side_effects=True, vmem_limit_bytes=50 * 1024 * 1024
         ),
         name="column_block",
-    )(lengths, flat(cotangent), flat(hidden), flat(latents), conv_two, conv_one)
-    out = masked + out
+    )(lengths, flat(cotangent), flat(hidden), flat(latents), in_hbm(conv_two), in_hbm(conv_one))
     return out.reshape(1, frames, rows, 1, ch)
 
 

time: 28 us -> 25.9 us (0.925)
  other arithmetic: 1.9 us -> 0 us
  Pallas kernels: 25.3 us -> 24.4 us
  local copies, waits for them, and re-layouts: 0 us -> 0.75 us
    add x1 -> x0, other arithmetic: 1.9 us -> none  [on_device(): out = masked + out]
    pallas_call x1, Pallas kernels: 25.3 us -> 24.4 us  [on_device(): pl.pallas_call(functools.partial(kernel, (tms, rws, fd, rd, cols, ch)), o...]
    unnamed x0 -> x1, local copies, waits for them, and re-layouts: none -> 0.75 us
where the time goes in v4:
time: 25.9 us; the launch traced here: 25.8 us
  Pallas kernels  24.4 us (94%)
  local copies, waits for them, and re-layouts  0.75 us (3%)
  between operations  0.66 us (3%)
    pallas_call x1, Pallas kernels, on_device(): pl.pallas_call(functools.partial(kernel, (tms, rws, fd, rd, cols, ch)), o...  24.4 us
    unnamed x1, local copies, waits for them, and re-layouts  0.75 us

profile of v4, /device:TPU:1, one launch (start us, length us, event | category | flops | bytes accessed | tf_op | source)
XLA Modules:
  0.0 25.8 jit_solution(14167576072301491267)
XLA Ops:
  0.7 24.4 %column_block.1 = f32[768,128]{1,0:T(8,128)S(1)} custom-call(s32[1]{0:T(128)S(6)} %copy.9.len_ref, bf16[256,384]{1,0:T(8,128)(2,1)} %bitcast.5, bf16[256,384]{1,0:T(8,128)(2,1)} %bitcast.6, bf16[256,384]{1,0:T(8,128)(2,1)} %bitcast.7, bf16[3,3,3,384,384]{4,3,2,1,0:T(8,128)(2,1)} %w_two.1, bf16[3,3,3,384,384]{4,3,2,1,0:T(8,128)(2,1)} %w_one.1), custom_call_target="tpu_custom_call" | custom-call | tf_op jit(solution)/shard_map/column_block/pallas_call | solution.py:288
  25.0 0.7 %copy.10 = f32[1,8,32,1,384]{4,3,2,1,0:T(1,128)} copy(f32[1,8,32,1,384]{4,3,2,1,0:T(1,128)S(1)} %bitcast.4) | data formatting | bytes 786432

commit v5 on v4

--- a/solution.py
+++ b/solution.py
@@ -34,11 +34,11 @@
     hid_in,
     lat_in,
     tmp,
-    tmp_back,
     stage_c,
     stage_h,
     stage_l,
     recv_c,
+    recv_o,
     recv_h,
     recv_l,
     cots,
@@ -50,6 +50,8 @@
     w_sem,
     c_send,
     c_recv,
+    o_send,
+    o_recv,
     h_send,
     h_recv,
     l_send,
@@ -120,14 +122,16 @@
 
         lax.fori_loop(0, cols, one, 0)
 
-    def pair_at(device):
-        return pl.ds(device + lax.rem(device, 2), 2)
-
-    def send_all(stage, recv, at, send_sem, recv_sem):
+    def outer_at(device):
+        return device + 2 * lax.rem(device, 2)
+
+    def send_all(stage, recv, at, send_sem, recv_sem, chans=None):
+        chans = pl.ds(0, ch) if chans is None else chans
+
         each_peer(
             lambda d_tm, d_rw: pltpu.make_async_remote_copy(
-                src_ref=stage.at[at(d_tm * rws + d_rw)],
-                dst_ref=recv.at[me],
+                src_ref=stage.at[at(d_tm * rws + d_rw), :, chans],
+                dst_ref=recv.at[me, :, chans],
                 send_sem=send_sem,
                 recv_sem=recv_sem,
                 device_id=(dp, d_tm, d_rw),
@@ -135,24 +139,28 @@
             ).start()
         )
 
-    def wait_all(recv, sem):
-        part = recv.at[pl.ds(0, group - 1)]
+    def wait_all(recv, sem, chans=None):
+        part = recv.at[pl.ds(0, group - 1), :, pl.ds(0, ch) if chans is None else chans]
         pltpu.make_async_copy(part, part, sem).wait()
 
     no_column = jnp.zeros((fd * rd, ch), BF16)
     stage_c[0] = no_column
     stage_c[cols + 1] = no_column
+    blocks = (pl.ds(0, SPLIT), pl.ds(SPLIT, ch - SPLIT))
     own_copies[0].wait()
     columns_of(cot_in, stage_c, 1, True)
     pl.semaphore_wait(barrier, group - 1)
-    send_all(stage_c, recv_c, pair_at, c_send, c_recv)
+    send_all(stage_c, recv_c, lambda device: device + 1, c_send, c_recv)
+    send_all(stage_c, recv_o, outer_at, o_send, o_recv)
     own_copies[1].wait()
     columns_of(hid_in, stage_h, 0, False)
-    send_all(stage_h, recv_h, lambda device: device, h_send, h_recv)
+    for at, chans in enumerate(blocks):
+        send_all(stage_h, recv_h, lambda device: device, h_send.at[at], h_recv.at[at], chans)
     own_copies[2].wait()
     columns_of(lat_in, stage_l, 0, False)
     send_all(stage_l, recv_l, lambda device: device, l_send, l_recv)
-    recv_c[me] = stage_c[pair_at(me)]
+    recv_c[me] = stage_c[me + 1]
+    recv_o[me] = stage_c[outer_at(me)]
     recv_h[me] = stage_h[me]
     recv_l[me] = stage_l[me]
 
@@ -164,15 +172,24 @@
     def _():
         grads[outer_slot, pl.ds(0, pix), :] = jnp.zeros((pix, ch), BF16)
 
-    def gather_rows(block):
+    def gather_rows(recv, write, chans=slice(None)):
         for t in range(tms):
-            for pair in range(rws // 2):
-                one = block(t * rws + 2 * pair).astype(F32)
-                two = block(t * rws + 2 * pair + 1).astype(F32)
-                for f in range(fd):
-                    joined = jnp.concatenate([one[f * rd : (f + 1) * rd], two[f * rd : (f + 1) * rd]], axis=0)
-                    start = (t * fd + f) * rows + 2 * pair * rd
-                    tmp_back[start : start + 2 * rd, :] = joined
+            for f in range(fd):
+                for first in range(0, rws, 4):
+                    parts = [recv[t * rws + first + i, f * rd : (f + 1) * rd, chans] for i in range(4)]
+                    write(pl.ds((t * fd + f) * rows + first * rd, 4 * rd), chans, jnp.concatenate(parts, axis=0))
+
+    def into(buf, slot):
+        def write(at, chans, block):
+            buf[slot, at, chans] = block
+
+        return write
+
+    def slope_into(buf):
+        def write(at, chans, block):
+            buf[at, chans] = silu_slope(block.astype(F32))
+
+        return write
 
     def copy_column(buf, chans, slot, target, send_sem, recv_sem):
         return pltpu.make_async_remote_copy(
@@ -193,12 +210,9 @@
         return copy_column(buf, chans, mate_slot, lax.rem(me + 2 * odd - 1 + group, group), *sems)
 
     wait_all(recv_c, c_recv)
-    gather_rows(lambda source: recv_c[source, 1 - odd])
-    cots[1, pl.ds(0, pix), :] = tmp_back[...].astype(BF16)
+    gather_rows(recv_c, into(cots, 1))
     mate_copy = to_mate(cots, pl.ds(0, ch), (x_sem.at[0], x_sem.at[1]))
     mate_copy.start()
-    gather_rows(lambda source: recv_c[source, odd])
-    cots[outer_slot, pl.ds(0, pix), :] = tmp_back[...].astype(BF16)
 
     def stacked(buf, columns, ins):
         parts = [buf[c, (2 - a) * rows : (2 - a) * rows + pix, ins] for c in columns for a in range(3)]
@@ -226,19 +240,20 @@
         down = jnp.where(at_row == 0, 0.0, pltpu.roll(below, 1, 0))
         return same + up + down
 
-    for copy in weight_copies[:3]:
+    weight_copies[0].wait()
+    acc[...] = product(cots, wv_two, (1,), every, every)
+    wait_all(recv_o, o_recv)
+    gather_rows(recv_o, into(cots, outer_slot))
+    for copy in weight_copies[1:3]:
         copy.wait()
+    mate_copy.wait_recv()
     g_copies = []
     for at, outs in enumerate((slice(0, SPLIT), slice(SPLIT, ch))):
         n = outs.stop - outs.start
-        acc[:, : 3 * n] = product(cots, wv_two, (1, outer_slot), outs, every)
-        if at == 0:
-            wait_all(recv_h, h_recv)
-            gather_rows(lambda source: recv_h[source])
-            slope_h[...] = silu_slope(tmp_back[...])
-            mate_copy.wait_recv()
-        part = product(cots, wv_two, (mate_slot,), outs, every)
-        taps = [acc[:, r * n : (r + 1) * n] + part[:, r * n : (r + 1) * n] for r in range(3)]
+        part = product(cots, wv_two, (mate_slot, outer_slot), outs, every)
+        taps = [acc[:, r * ch + outs.start : r * ch + outs.stop] + part[:, r * n : (r + 1) * n] for r in range(3)]
+        wait_all(recv_h, h_recv.at[at], blocks[at])
+        gather_rows(recv_h, slope_into(slope_h), outs)
         grads[1, pl.ds(0, pix), outs] = (row_taps(*taps) * slope_h[:, outs]).astype(BF16)
         chans = pl.ds(outs.start, n)
         outer = to_outer(grads, chans, (g_sem.at[at, 0], g_sem.at[at, 1]))
@@ -254,8 +269,7 @@
         mate.wait_recv()
     acc[...] += product(grads, wv_one, (mate_slot,), every, every)
     wait_all(recv_l, l_recv)
-    gather_rows(lambda source: recv_l[source])
-    slope_l[...] = silu_slope(tmp_back[...])
+    gather_rows(recv_l, slope_into(slope_l))
     pl.when(inner)(g_copies[0][0].wait_recv)
     acc[...] += product(grads, wv_one, (outer_slot,), every, slice(0, SPLIT))
     pl.when(inner)(g_copies[1][0].wait_recv)
@@ -266,7 +280,9 @@
         out_ref[pl.ds(j, pix, stride=strips), :] = result[:, j * lanes : (j + 1) * lanes]
 
     wait_all(recv_c, c_send)
-    wait_all(recv_h, h_send)
+    wait_all(recv_o, o_send)
+    for at, chans in enumerate(blocks):
+        wait_all(recv_h, h_send.at[at], chans)
     wait_all(recv_l, l_send)
     mate_copy.wait_send()
     for outer, mate in g_copies:
@@ -295,11 +311,9 @@
             pltpu.VMEM(conv_one.shape, BF16),
             *[pltpu.VMEM((local, ch), BF16)] * 3,
             pltpu.VMEM((ch // 128, local, 128), F32),
-            pltpu.VMEM((pix, ch), F32),
             pltpu.VMEM((cols + 2, fd * rd, ch), BF16),
             *[pltpu.VMEM((cols, fd * rd, ch), BF16)] * 2,
-            pltpu.VMEM((group, 2, fd * rd, ch), BF16),
-            *[pltpu.VMEM((group, fd * rd, ch), BF16)] * 2,
+            *[pltpu.VMEM((group, fd * rd, ch), BF16)] * 4,
             pltpu.VMEM((3, pix + 2 * rows, ch), BF16),
             pltpu.VMEM((3, pix + 2 * rows, ch), BF16),
             pltpu.VMEM((pix, 3 * ch), F32),
@@ -307,7 +321,9 @@
             pltpu.VMEM((pix, ch), F32),
             dma((3,)),
             dma((2, 3)),
-            *[dma] * 6,
+            *[dma] * 4,
+            *[dma((2,))] * 2,
+            *[dma] * 2,
             dma((2,)),
             dma((2, 4)),
         ],

time: 25.9 us -> 23.8 us (0.919)
  Pallas kernels: 24.4 us -> 22.2 us
    pallas_call x1, Pallas kernels: 24.4 us -> 22.2 us  [on_device(): pl.pallas_call(functools.partial(kernel, (tms, rws, fd, rd, cols, ch)), o...]
where the time goes in v5:
time: 23.8 us; the launch traced here: 23.6 us
  Pallas kernels  22.2 us (93%)
  local copies, waits for them, and re-layouts  0.75 us (3%)
  between operations  0.66 us (3%)
    pallas_call x1, Pallas kernels, on_device(): pl.pallas_call(functools.partial(kernel, (tms, rws, fd, rd, cols, ch)), o...  22.2 us
    unnamed x1, local copies, waits for them, and re-layouts  0.75 us

profile of v5, /device:TPU:1, one launch (start us, length us, event | category | flops | bytes accessed | tf_op | source)
XLA Modules:
  0.0 23.6 jit_solution(9814010330873031914)
XLA Ops:
  0.7 22.2 %column_block.1 = f32[768,128]{1,0:T(8,128)S(1)} custom-call(s32[1]{0:T(128)S(6)} %copy.9.len_ref, bf16[256,384]{1,0:T(8,128)(2,1)} %bitcast.5, bf16[256,384]{1,0:T(8,128)(2,1)} %bitcast.6, bf16[256,384]{1,0:T(8,128)(2,1)} %bitcast.7, bf16[3,3,3,384,384]{4,3,2,1,0:T(8,128)(2,1)} %w_two.1, bf16[3,3,3,384,384]{4,3,2,1,0:T(8,128)(2,1)} %w_one.1), custom_call_target="tpu_custom_call" | custom-call | tf_op jit(solution)/shard_map/column_block/pallas_call | solution.py:304
  22.9 0.7 %copy.10 = f32[1,8,32,1,384]{4,3,2,1,0:T(1,128)} copy(f32[1,8,32,1,384]{4,3,2,1,0:T(1,128)S(1)} %bitcast.4) | data formatting | bytes 786432

commit v6 on v5

--- a/solution.py
+++ b/solution.py
@@ -44,7 +44,7 @@
     cots,
     grads,
     acc,
-    slope_h,
+    partial,
     slope_l,
     in_sem,
     w_sem,
@@ -72,15 +72,22 @@
     mate_slot = 2 * odd
     outer_slot = 2 - 2 * odd
 
+    chip = rw - odd
+    chips = rws // 2
+
     def each_peer(action):
-        for step in sorted(range(tms), key=lambda s: -min(s, tms - s)):
+        for step in sorted(range(chips), key=lambda s: -min(s, chips - s)):
 
             def one(k, carry, step=step):
-                turn = k if step == 0 else lax.rem(k + rws // 2 - 1, rws)
-                action(lax.rem(tm + step, tms), lax.rem(rw + turn, rws))
+                if step == 0:
+                    action(lax.rem(tm + k // 2, tms), chip + lax.rem(odd + k, 2))
+                else:
+                    action(
+                        lax.rem(tm + k // 2 + tms // 2, tms), lax.rem(chip + 2 * step + lax.rem(k, 2), rws)
+                    )
                 return carry
 
-            lax.fori_loop(1 if step == 0 else 0, rws, one, 0)
+            lax.fori_loop(1 if step == 0 else 0, 2 * tms, one, 0)
 
     own_copies = []
     for n, (src, dst) in enumerate(((cot_ref, cot_in), (hid_ref, hid_in), (lat_ref, lat_in))):
@@ -185,6 +192,12 @@
 
         return write
 
+    def scaled_into(buf):
+        def write(at, chans, block):
+            buf[1, at, chans] = (partial[at, chans] * silu_slope(block.astype(F32))).astype(BF16)
+
+        return write
+
     def slope_into(buf):
         def write(at, chans, block):
             buf[at, chans] = silu_slope(block.astype(F32))
@@ -239,6 +252,19 @@
         up = jnp.where(at_row == rows - 1, 0.0, pltpu.roll(above, pix - 1, 0))
         down = jnp.where(at_row == 0, 0.0, pltpu.roll(below, 1, 0))
         return same + up + down
+
+    def shifted_product(buf, wv, column, ins):
+        block = buf[column, :, ins].astype(F32)
+        size = block.shape[0]
+        at_row = lax.rem(lax.broadcasted_iota(jnp.int32, block.shape, 0), rows)
+        above = jnp.where(at_row == rows - 1, 0.0, pltpu.roll(block, size - 1, 0))
+        below = jnp.where(at_row == 0, 0.0, pltpu.roll(block, 1, 0))
+        taps = [tap.astype(BF16) for tap in (above, block, below)]
+        left = [taps[r][(2 - a) * rows : (2 - a) * rows + pix] for r in range(3) for a in range(3)]
+        right = [wv[a, r, column, :, ins] for r in range(3) for a in range(3)]
+        return lax.dot_general(
+            jnp.concatenate(left, axis=1), jnp.concatenate(right, axis=1), NT, preferred_element_type=F32
+        )
 
     weight_copies[0].wait()
     acc[...] = product(cots, wv_two, (1,), every, every)
@@ -252,9 +278,10 @@
         n = outs.stop - outs.start
         part = product(cots, wv_two, (mate_slot, outer_slot), outs, every)
         taps = [acc[:, r * ch + outs.start : r * ch + outs.stop] + part[:, r * n : (r + 1) * n] for r in range(3)]
+        partial[:, outs] = row_taps(*taps)
         wait_all(recv_h, h_recv.at[at], blocks[at])
-        gather_rows(recv_h, slope_into(slope_h), outs)
-        grads[1, pl.ds(0, pix), outs] = (row_taps(*taps) * slope_h[:, outs]).astype(BF16)
+        gather_rows(recv_h, slope_into(slope_l), outs)
+        grads[1, pl.ds(0, pix), outs] = (partial[:, outs] * slope_l[:, outs]).astype(BF16)
         chans = pl.ds(outs.start, n)
         outer = to_outer(grads, chans, (g_sem.at[at, 0], g_sem.at[at, 1]))
         mate = to_mate(grads, chans, (g_sem.at[at, 2], g_sem.at[at, 3]))
@@ -267,9 +294,9 @@
     acc[...] = product(grads, wv_one, (1,), every, every)
     for _, mate in g_copies:
         mate.wait_recv()
-    acc[...] += product(grads, wv_one, (mate_slot,), every, every)
     wait_all(recv_l, l_recv)
     gather_rows(recv_l, slope_into(slope_l))
+    acc[...] += product(grads, wv_one, (mate_slot,), every, every)
     pl.when(inner)(g_copies[0][0].wait_recv)
     acc[...] += product(grads, wv_one, (outer_slot,), every, slice(0, SPLIT))
     pl.when(inner)(g_copies[1][0].wait_recv)

time: 23.8 us -> 23.3 us (0.979)
  Pallas kernels: 22.2 us -> 21.6 us
    pallas_call x1, Pallas kernels: 22.2 us -> 21.6 us  [on_device(): pl.pallas_call(functools.partial(kernel, (tms, rws, fd, rd, cols, ch)), o...]
where the time goes in v6:
time: 23.3 us; the launch traced here: 23 us
  Pallas kernels  21.6 us (93%)
  local copies, waits for them, and re-layouts  0.75 us (3%)
  between operations  0.66 us (3%)
    pallas_call x1, Pallas kernels, on_device(): pl.pallas_call(functools.partial(kernel, (tms, rws, fd, rd, cols, ch)), o...  21.6 us
    unnamed x1, local copies, waits for them, and re-layouts  0.75 us

profile of v6, /device:TPU:1, one launch (start us, length us, event | category | flops | bytes accessed | tf_op | source)
XLA Modules:
  0.0 23.0 jit_solution(17023557388267387765)
XLA Ops:
  0.7 21.6 %column_block.1 = f32[768,128]{1,0:T(8,128)S(1)} custom-call(s32[1]{0:T(128)S(6)} %copy.9.len_ref, bf16[256,384]{1,0:T(8,128)(2,1)} %bitcast.5, bf16[256,384]{1,0:T(8,128)(2,1)} %bitcast.6, bf16[256,384]{1,0:T(8,128)(2,1)} %bitcast.7, bf16[3,3,3,384,384]{4,3,2,1,0:T(8,128)(2,1)} %w_two.1, bf16[3,3,3,384,384]{4,3,2,1,0:T(8,128)(2,1)} %w_one.1), custom_call_target="tpu_custom_call" | custom-call | tf_op jit(solution)/shard_map/column_block/pallas_call | solution.py:331
  22.3 0.7 %copy.10 = f32[1,8,32,1,384]{4,3,2,1,0:T(1,128)} copy(f32[1,8,32,1,384]{4,3,2,1,0:T(1,128)S(1)} %bitcast.4) | data formatting | bytes 786432

commit v7 on v6

--- a/solution.py
+++ b/solution.py
@@ -268,15 +268,18 @@
 
     weight_copies[0].wait()
     acc[...] = product(cots, wv_two, (1,), every, every)
-    wait_all(recv_o, o_recv)
-    gather_rows(recv_o, into(cots, outer_slot))
     for copy in weight_copies[1:3]:
         copy.wait()
     mate_copy.wait_recv()
+    early = product(cots, wv_two, (mate_slot,), slice(0, SPLIT), every)
+    for r in range(3):
+        acc[:, r * ch : r * ch + SPLIT] += early[:, r * SPLIT : (r + 1) * SPLIT]
+    wait_all(recv_o, o_recv)
+    gather_rows(recv_o, into(cots, outer_slot))
     g_copies = []
     for at, outs in enumerate((slice(0, SPLIT), slice(SPLIT, ch))):
         n = outs.stop - outs.start
-        part = product(cots, wv_two, (mate_slot, outer_slot), outs, every)
+        part = product(cots, wv_two, (outer_slot,) if at == 0 else (mate_slot, outer_slot), outs, every)
         taps = [acc[:, r * ch + outs.start : r * ch + outs.stop] + part[:, r * n : (r + 1) * n] for r in range(3)]
         partial[:, outs] = row_taps(*taps)
         wait_all(recv_h, h_recv.at[at], blocks[at])

time: 23.3 us -> 23.3 us (level)
  no operation moved by 1% of the time
where the time goes in v7:
time: 23.3 us; the launch traced here: 23.1 us
  Pallas kernels  21.7 us (93%)
  local copies, waits for them, and re-layouts  0.75 us (3%)
  between operations  0.66 us (3%)
    pallas_call x1, Pallas kernels, on_device(): pl.pallas_call(functools.partial(kernel, (tms, rws, fd, rd, cols, ch)), o...  21.7 us
    unnamed x1, local copies, waits for them, and re-layouts  0.75 us

profile of v7, /device:TPU:1, one launch (start us, length us, event | category | flops | bytes accessed | tf_op | source)
XLA Modules:
  0.0 23.1 jit_solution(11759851907768147144)
XLA Ops:
  0.7 21.7 %column_block.1 = f32[768,128]{1,0:T(8,128)S(1)} custom-call(s32[1]{0:T(128)S(6)} %copy.9.len_ref, bf16[256,384]{1,0:T(8,128)(2,1)} %bitcast.5, bf16[256,384]{1,0:T(8,128)(2,1)} %bitcast.6, bf16[256,384]{1,0:T(8,128)(2,1)} %bitcast.7, bf16[3,3,3,384,384]{4,3,2,1,0:T(8,128)(2,1)} %w_two.1, bf16[3,3,3,384,384]{4,3,2,1,0:T(8,128)(2,1)} %w_one.1), custom_call_target="tpu_custom_call" | custom-call | tf_op jit(solution)/shard_map/column_block/pallas_call | solution.py:334
  22.4 0.7 %copy.10 = f32[1,8,32,1,384]{4,3,2,1,0:T(1,128)} copy(f32[1,8,32,1,384]{4,3,2,1,0:T(1,128)S(1)} %bitcast.4) | data formatting | bytes 786432

commit v8 on v7

--- a/solution.py
+++ b/solution.py
@@ -119,15 +119,12 @@
         for j in range(strips):
             tmp[j] = src_ref[:, j * lanes : (j + 1) * lanes].astype(F32)
 
-        def one(w, carry):
+        for w in range(cols):
             for j in range(strips):
                 block = tmp.at[j][pl.ds(w, fd * rd, stride=cols), :]
                 if masked:
                     block = jnp.where(live, block, 0.0)
                 dst_ref[first + w, :, j * lanes : (j + 1) * lanes] = block.astype(BF16)
-            return carry
-
-        lax.fori_loop(0, cols, one, 0)
 
     def outer_at(device):
         return device + 2 * lax.rem(device, 2)

time: 23.3 us -> 23.3 us (level)
  no operation moved by 1% of the time
where the time goes in v8:
time: 23.3 us; the launch traced here: 23.1 us
  Pallas kernels  21.7 us (93%)
  local copies, waits for them, and re-layouts  0.75 us (3%)
  between operations  0.66 us (3%)
    pallas_call x1, Pallas kernels, on_device(): pl.pallas_call(functools.partial(kernel, (tms, rws, fd, rd, cols, ch)), o...  21.7 us
    unnamed x1, local copies, waits for them, and re-layouts  0.75 us

profile of v8, /device:TPU:1, one launch (start us, length us, event | category | flops | bytes accessed | tf_op | source)
XLA Modules:
  0.0 23.1 jit_solution(6804302503318843194)
XLA Ops:
  0.7 21.7 %column_block.1 = f32[768,128]{1,0:T(8,128)S(1)} custom-call(s32[1]{0:T(128)S(6)} %copy.9.len_ref, bf16[256,384]{1,0:T(8,128)(2,1)} %bitcast.5, bf16[256,384]{1,0:T(8,128)(2,1)} %bitcast.6, bf16[256,384]{1,0:T(8,128)(2,1)} %bitcast.7, bf16[3,3,3,384,384]{4,3,2,1,0:T(8,128)(2,1)} %w_two.1, bf16[3,3,3,384,384]{4,3,2,1,0:T(8,128)(2,1)} %w_one.1), custom_call_target="tpu_custom_call" | custom-call | tf_op jit(solution)/shard_map/column_block/pallas_call | solution.py:331
  22.4 0.7 %copy.10 = f32[1,8,32,1,384]{4,3,2,1,0:T(1,128)} copy(f32[1,8,32,1,384]{4,3,2,1,0:T(1,128)S(1)} %bitcast.4) | data formatting | bytes 786432

commit v9 on v8

--- a/solution.py
+++ b/solution.py
@@ -297,6 +297,12 @@
     wait_all(recv_l, l_recv)
     gather_rows(recv_l, slope_into(slope_l))
     acc[...] += product(grads, wv_one, (mate_slot,), every, every)
+    wait_all(recv_c, c_send)
+    wait_all(recv_o, o_send)
+    for at, chans in enumerate(blocks):
+        wait_all(recv_h, h_send.at[at], chans)
+    wait_all(recv_l, l_send)
+    mate_copy.wait_send()
     pl.when(inner)(g_copies[0][0].wait_recv)
     acc[...] += product(grads, wv_one, (outer_slot,), every, slice(0, SPLIT))
     pl.when(inner)(g_copies[1][0].wait_recv)
@@ -306,12 +312,6 @@
     for j in range(strips):
         out_ref[pl.ds(j, pix, stride=strips), :] = result[:, j * lanes : (j + 1) * lanes]
 
-    wait_all(recv_c, c_send)
-    wait_all(recv_o, o_send)
-    for at, chans in enumerate(blocks):
-        wait_all(recv_h, h_send.at[at], chans)
-    wait_all(recv_l, l_send)
-    mate_copy.wait_send()
     for outer, mate in g_copies:
         pl.when(inner)(outer.wait_send)
         mate.wait_send()

time: 23.3 us -> 23.2 us (level)
  no operation moved by 1% of the time
where the time goes in v9:
time: 23.2 us; the launch traced here: 23.1 us
  Pallas kernels  21.7 us (94%)
  local copies, waits for them, and re-layouts  0.75 us (3%)
  between operations  0.66 us (3%)
    pallas_call x1, Pallas kernels, on_device(): pl.pallas_call(functools.partial(kernel, (tms, rws, fd, rd, cols, ch)), o...  21.7 us
    unnamed x1, local copies, waits for them, and re-layouts  0.75 us

profile of v9, /device:TPU:1, one launch (start us, length us, event | category | flops | bytes accessed | tf_op | source)
XLA Modules:
  0.0 23.1 jit_solution(13651399315117297940)
XLA Ops:
  0.7 21.7 %column_block.1 = f32[768,128]{1,0:T(8,128)S(1)} custom-call(s32[1]{0:T(128)S(6)} %copy.9.len_ref, bf16[256,384]{1,0:T(8,128)(2,1)} %bitcast.5, bf16[256,384]{1,0:T(8,128)(2,1)} %bitcast.6, bf16[256,384]{1,0:T(8,128)(2,1)} %bitcast.7, bf16[3,3,3,384,384]{4,3,2,1,0:T(8,128)(2,1)} %w_two.1, bf16[3,3,3,384,384]{4,3,2,1,0:T(8,128)(2,1)} %w_one.1), custom_call_target="tpu_custom_call" | custom-call | tf_op jit(solution)/shard_map/column_block/pallas_call | solution.py:331
  22.4 0.7 %copy.10 = f32[1,8,32,1,384]{4,3,2,1,0:T(1,128)} copy(f32[1,8,32,1,384]{4,3,2,1,0:T(1,128)S(1)} %bitcast.4) | data formatting | bytes 786432
